TPU v7x, 512 devices: a whole 4x8x8 slice. The times are simulated.
512 devices in a mesh: kv: 8 (over x, core), seq: 64 (over z, y).
Axes of the slice: x: 4, y: 8, z: 8, core: 2. Of those that a mesh axis runs over, the one named last changes fastest.
Arguments:
- queries: bfloat16 [512, 4096], P(('kv', 'seq')), may hold values from -6 to 6
- out_grad: bfloat16 [512, 4096], P(('kv', 'seq')), may hold values from -3072 to 3072
- saved_out: bfloat16 [512, 4096], P(('kv', 'seq')), may hold values from -1.5 to 1.5
- saved_lse: float32 [512, 32], P(('kv', 'seq')), as said below
- video_keys: bfloat16 [16384, 1024], P('seq', 'kv'), may hold values from -6 to 6
- video_values: bfloat16 [16384, 1024], P('seq', 'kv'), may hold values from -6 to 6
Outputs:
- grad_queries: bfloat16 [512, 4096], P(('kv', 'seq'))
- grad_keys: bfloat16 [16384, 1024], P('seq', 'kv')
- grad_values: bfloat16 [16384, 1024], P('seq', 'kv')
Inputs may be any that keep to these rules, and one draw needn't show every extreme that they name: saved_lse lies between log(16384) and log(16384) + 1.5.
All inputs are finite; a program needn't handle non-finite values.
Results may differ from a plain program's by a relative error of at most 0.0057.
Values may be sent and summed in bfloat16 or wider, within the bound.
A program may use at most 64 MiB of HBM per device.

v0:
```python
import math

import jax
import jax.numpy as jnp
from jax import lax
from jax.sharding import PartitionSpec as P


def head_columns(block, first, width):
    return lax.dynamic_slice_in_dim(block, first, width, 1)


def seq_major(block, kv_count, seq_count):
    total_rows = block.shape[0]
    width = block.shape[1]
    shaped = block.reshape(kv_count, seq_count, total_rows // (kv_count * seq_count), width)
    return shaped.transpose(1, 0, 2, 3).reshape(total_rows, width)


def make_accumulate(
    lse_group,
    delta_group,
    group_index,
    group_width,
    group_heads,
    head_width,
    score_scale,
    video_keys,
    video_values,
):

    def accumulate(totals, pieces, offset):
        key_total, value_total, query_rows = totals
        query_block, grad_block = pieces
        query_block = head_columns(query_block, group_index * group_width, group_width)
        grad_block = head_columns(grad_block, group_index * group_width, group_width)
        columns = []
        for member in range(group_heads):
            query_head = query_block[:, member * head_width : (member + 1) * head_width]
            grad_head = grad_block[:, member * head_width : (member + 1) * head_width]
            scores = (
                jnp.einsum("nd,kd->nk", query_head, video_keys, preferred_element_type=jnp.float32)
                * score_scale
            )
            probs = jnp.exp(scores - lse_group[:, member : member + 1])
            probs_half = probs.astype(jnp.bfloat16)
            value_total = value_total + jnp.einsum(
                "nk,nd->kd", probs_half, grad_head, preferred_element_type=jnp.float32
            )
            dprobs = jnp.einsum(
                "nd,kd->nk", grad_head, video_values, preferred_element_type=jnp.float32
            )
            dscores = (probs * (dprobs - delta_group[:, member : member + 1])).astype(jnp.bfloat16)
            key_total = key_total + jnp.einsum(
                "nk,nd->kd", dscores, query_head, preferred_element_type=jnp.float32
            )
            columns.append(
                jnp.einsum("nk,kd->nd", dscores, video_keys, preferred_element_type=jnp.float32)
            )
        query_rows = jnp.concatenate(columns, axis=1)
        return (key_total, value_total, query_rows)

    return accumulate


def shards(queries, out_grad, saved_out, saved_lse, video_keys, video_values):
    kv_count = lax.axis_size("kv")
    seq_count = lax.axis_size("seq")
    group_index = lax.axis_index("kv")
    head_width = video_keys.shape[1]
    group_heads = saved_lse.shape[1] // kv_count
    group_width = group_heads * head_width
    own_rows = queries.shape[0]
    total_rows = own_rows * kv_count * seq_count
    score_scale = 1.0 / math.sqrt(head_width)
    products = out_grad.astype(jnp.float32) * saved_out.astype(jnp.float32)
    own_delta = products.reshape(own_rows, -1, head_width).sum(axis=2)
    lse_all, delta_all = (
        lax.all_gather(saved_lse, ("kv", "seq"), axis=0, tiled=True),
        lax.all_gather(own_delta, ("kv", "seq"), axis=0, tiled=True),
    )
    lse_wide = head_columns(lse_all, group_index * group_heads, group_heads)
    delta_wide = head_columns(delta_all, group_index * group_heads, group_heads)
    key_rows = video_keys.shape[0]
    initial = (
        jnp.zeros((key_rows, head_width), jnp.float32),
        jnp.zeros((key_rows, head_width), jnp.float32),
        jnp.zeros((total_rows, group_width), jnp.float32),
    )
    wide_step = make_accumulate(
        lse_wide,
        delta_wide,
        group_index,
        group_width,
        group_heads,
        head_width,
        score_scale,
        video_keys,
        video_values,
    )
    gathered = (
        lax.all_gather(queries, ("kv", "seq"), axis=0, tiled=True),
        lax.all_gather(out_grad, ("kv", "seq"), axis=0, tiled=True),
    )
    key_total, value_total, query_rows = wide_step(initial, gathered, 0)
    query_rows = seq_major(query_rows, kv_count, seq_count)
    summed = lax.psum_scatter(
        query_rows.reshape(seq_count, total_rows // seq_count, group_width),
        "seq",
        scatter_dimension=0,
        tiled=True,
    )
    rounded = (summed * score_scale).astype(jnp.bfloat16).reshape(kv_count, own_rows, group_width)
    returned = lax.all_to_all(rounded, "kv", split_axis=0, concat_axis=2, tiled=True)
    grad_queries = returned.reshape(own_rows, kv_count * group_width)
    return (
        grad_queries,
        (key_total * score_scale).astype(jnp.bfloat16),
        value_total.astype(jnp.bfloat16),
    )


def solution(mesh):
    return jax.shard_map(
        shards,
        mesh=mesh,
        in_specs=(
            P(("kv", "seq"), None),
            P(("kv", "seq"), None),
            P(("kv", "seq"), None),
            P(("kv", "seq"), None),
            P("seq", "kv"),
            P("seq", "kv"),
        ),
        out_specs=(P(("kv", "seq"), None), P("seq", "kv"), P("seq", "kv")),
        check_vma=False,
    )
```

profile of v0, /device:TPU:1, one launch (start us, length us, event | category | flops | bytes accessed | tf_op | source)
XLA Modules:
  0.0 824.8 jit_solution(11572126414588842598)
XLA Ops:
  7.2 0.8 convert_multiply_fusion
  8.1 0.3 dynamic-update-slice
  8.4 0.8 reshape.27
  9.3 0.7 all-gather.7.cloned.1.call-update
  10.1 0.7 all-gather.9.cloned.1.call-update
  10.8 66.6 %all-gather.2 = f32[512,1,32]{2,1,0:T(1,128)S(1)} all-gather(f32[1,1,32]{2,1,0:T(1,128)} %bitcast.70), channel_id=1, replica_groups=mesh['kv'=8,'seq'=64] {'kv','seq'}, dimensions={0}, use_global_device_ids=true | all-gather | bytes 65664 | tf_op jit(solution)/shard_map/all_gather | solution.py:79
  77.4 0.6 constant_dynamic-slice_fusion.1
  78.1 212.3 %all-reduce.5.cloned.1.call-done = f32[512,32]{1,0:T(8,128)} async-done(((f32[512,32]{1,0:T(8,128)}), f32[512,32]{1,0:T(8,128)}) %all-reduce.5.cloned.1.call-update) | async-done | bytes 65552
  290.5 2.0 dynamic-slice_reduce_fusion.3
  292.5 127.6 %all-gather.7.cloned.1.call-done = bf16[512,1,4096]{2,1,0:T(2,128)(2,1)} async-done(((bf16[1,1,4096]{2,1,0:T(2,128)(2,1)}), bf16[512,1,4096]{2,1,0:T(2,128)(2,1)}) %all-gather.7.cloned.1.call-update) | async-done | bytes 4194320 | tf_op jit(solution)/shard_map/all_gather | solution.py:102
  420.0 2.3 constant_dynamic-slice_fusion.2
  422.3 0.1 copy.24
  422.5 126.2 %all-gather.9.cloned.1.call-done = bf16[512,1,4096]{2,1,0:T(2,128)(2,1)} async-done(((bf16[1,1,4096]{2,1,0:T(2,128)(2,1)}), bf16[512,1,4096]{2,1,0:T(2,128)(2,1)}) %all-gather.9.cloned.1.call-update) | async-done | bytes 4194320 | tf_op jit(solution)/shard_map/all_gather | solution.py:103
  548.7 2.3 constant_dynamic-slice_fusion
  551.0 0.1 copy.23
  551.1 0.2 fusion.10
  551.4 0.2 fusion.12
  551.6 0.2 fusion.46
  551.8 0.2 fusion.7
  552.1 0.2 fusion.13
  552.3 0.2 fusion.45
  552.6 0.2 fusion.4
  552.8 0.2 fusion.14
  553.1 0.2 fusion.44
  553.3 0.4 copy-done.2
  553.8 0.2 fusion.1
  554.0 0.2 fusion.15
  554.3 0.7 copy-done.3
  555.0 0.2 fusion.43
  555.2 1.1 pad_maximum_fusion
  556.3 2.6 copy.16
  558.9 2.8 copy.17
  561.7 1.2 fusion.38
  562.9 1.2 convolution_add_fusion.5
  564.2 1.9 convolution_add_fusion.4
  566.0 0.3 fusion.22
  566.3 0.3 convolution_add_fusion.2
  566.6 0.3 convolution_add_fusion.1
  566.8 0.9 fusion.18
  567.7 233.1 %reduce-scatter.4.cloned.1.call-done = f32[1,8,512]{2,1,0:T(8,128)} async-done(((f32[64,8,512]{2,1,0:T(8,128)}), f32[1,8,512]{2,1,0:T(8,128)}) %reduce-scatter.4.cloned.1.call-update) | async-done | bytes 16400
  800.9 0.7 fusion.41
  801.6 0.5 broadcast.13
  802.1 0.6 reduce.9
  802.8 0.6 reshape.44
  803.4 9.7 %all-to-all-start = ((bf16[8,2,256]{2,1,0:T(2,128)(2,1)}), bf16[8,2,256]{2,1,0:T(2,128)(2,1)S(1)}, u32[]{:S(2)}, u32[]{:S(2)}) async-start(bf16[8,2,256]{2,1,0:T(2,128)(2,1)} %reshape.44), calls=%async_computation | async-start | bytes 16384 | tf_op jit(solution)/shard_map/all_to_all | solution.py:114
  813.0 1.8 fusion.17
  814.9 2.8 all-to-all-done
  817.7 0.6 reshape.45
  (18 shorter events, 0.5 us)
Async XLA Ops:
  7.2 543.9 %copy-start = (bf16[256,128]{1,0:T(8,128)(2,1)S(1)}, bf16[256,128]{1,0:T(8,128)(2,1)}, u32[]{:S(2)}) copy-start(bf16[256,128]{1,0:T(8,128)(2,1)} %param.10) | copy-start | bytes 196612
  7.2 544.2 %copy-start.4 = (bf16[256,128]{1,0:T(8,128)(2,1)S(1)}, bf16[256,128]{1,0:T(8,128)(2,1)}, u32[]{:S(2)}) copy-start(bf16[256,128]{1,0:T(8,128)(2,1)} %param.11) | copy-start | bytes 196612
  7.2 283.3 %all-reduce.5.cloned.1.call-start = ((), (), s32[]{:S(2)}) async-start(), calls=%async_computation.4 | async-start | bytes 524288
  9.3 410.8 %all-gather.7.cloned.1.call-start = ((), (), s32[]{:S(2)}) async-start(), calls=%async_computation.2 | async-start | bytes 8404992 | tf_op jit(solution)/shard_map/all_gather | solution.py:102
  10.0 538.6 %all-gather.9.cloned.1.call-start = ((), (), s32[]{:S(2)}) async-start(), calls=%async_computation.3 | async-start | bytes 8404992 | tf_op jit(solution)/shard_map/all_gather | solution.py:103
  10.7 790.1 %reduce-scatter.4.cloned.1.call-start = ((), (), s32[]{:S(2)}) async-start(), calls=%async_computation.5 | async-start | bytes 1064960
  552.3 1.0 copy-start.1
  553.1 0.7 copy-start.2
  554.3 0.7 copy-start.3
  803.4 14.3 %all-to-all-start = ((bf16[8,2,256]{2,1,0:T(2,128)(2,1)}), bf16[8,2,256]{2,1,0:T(2,128)(2,1)S(1)}, u32[]{:S(2)}, u32[]{:S(2)}) async-start(bf16[8,2,256]{2,1,0:T(2,128)(2,1)} %reshape.44), calls=%async_computation | async-start | bytes 16384 | tf_op jit(solution)/shard_map/all_to_all | solution.py:114
Sparse Core Ops, SparseCore 0:
  13.0 277.4 all-reduce.4
  294.9 125.1 all-gather.6
  424.5 124.1 all-gather.8
  561.8 239.0 reduce-scatter.3
where the time goes:
time: 825 us
  waiting for transfers between devices  703 us (85%)
  blocking collectives  66.6 us (8%)
  local copies, waits for them, and re-layouts  17 us (2%)
  between operations  14 us (2%)
  matrix products  10.7 us (1%)
  starting transfers between devices  9.82 us (1%)
    unnamed x6, waiting for transfers between devices  447 us
    all_gather x1, waiting for transfers between devices, shards(): lax.all_gather(queries, ('kv', 'seq'), axis=0, tiled=True)  128 us
    all_gather x1, waiting for transfers between devices, shards(): lax.all_gather(out_grad, ('kv', 'seq'), axis=0, tiled=True)  126 us
    all_gather x1, blocking collectives, shards(): lax.all_gather(saved_lse, ('kv', 'seq'), axis=0, tiled=True)  66.6 us
  transfers between devices with their start and end apart: 5, of which 5 were waited for; matrix products, arithmetic and copies ran while one was open for 2% of the time, Pallas kernels for 0%

commit v1 on v0

v1 whole, which is shorter than its diff:
```python
import functools
import math

import jax
import jax.numpy as jnp
from jax import lax
from jax.experimental import pallas as pl
from jax.experimental.pallas import tpu as pltpu
from jax.sharding import PartitionSpec as P

MESH = pl.DeviceIdType.MESH
LANES = 128


def other_coords(count):
    return sorted(range(1, count), key=lambda d: (min(d, count - d), d))


def kernel(
    sizes,
    q_ref,
    grad_ref,
    out_ref,
    lse_ref,
    keys_ref,
    values_ref,
    dq_ref,
    dkeys_ref,
    dvalues_ref,
    packet,
    packet_aux,
    got,
    got_aux,
    held0,
    held1,
    block0,
    block1,
    aux0,
    aux1,
    terms0,
    terms1,
    away0,
    away1,
    come0,
    come1,
    turned0,
    turned1,
    dq_away0,
    dq_away1,
    dq_come0,
    dq_come1,
    back,
    back_come,
    load_sem,
    exchange_send,
    exchange_recv,
    ring_send,
    ring_recv,
    block_send,
    block_recv,
    sum_send,
    sum_recv,
    dq_send,
    dq_recv,
    back_send,
    back_recv,
):
    groups, ny, nz, heads, width, half_keys = sizes
    counts = (ny, nz)
    held, block, aux = (held0, held1), (block0, block1), (aux0, aux1)
    terms, away, come = (terms0, terms1), (away0, away1), (come0, come1)
    turned = (turned0, turned1)
    dq_away, dq_come = (dq_away0, dq_away1), (dq_come0, dq_come1)
    pairs = groups * heads
    scale = 1.0 / math.sqrt(width)

    mine = lax.axis_index("kv")
    place = lax.axis_index("seq")
    y, z = lax.rem(place, ny), lax.div(place, ny)
    position = (y, z)

    def peer(axis, index):
        return (mine, z * ny + index) if axis == 0 else (mine, index * ny + y)

    def around(axis, step):
        return lax.rem(position[axis] + (step % counts[axis]), counts[axis])

    def remote(src, dst, send, recv, device):
        return pltpu.make_async_remote_copy(
            src_ref=src, dst_ref=dst, send_sem=send, recv_sem=recv, device_id=device, device_id_type=MESH
        )

    barrier = pltpu.get_barrier_semaphore()
    for d in range(1, groups):
        pl.semaphore_signal(barrier, inc=1, device_id=(lax.rem(mine + d, groups), place), device_id_type=MESH)
    for axis in (0, 1):
        for d in range(1, counts[axis]):
            pl.semaphore_signal(barrier, inc=1, device_id=peer(axis, around(axis, d)), device_id_type=MESH)

    loads = []
    for half in (0, 1):
        for part, source in ((0, keys_ref), (1, values_ref)):
            copy = pltpu.make_async_copy(
                source.at[pl.ds(half * half_keys, half_keys), :],
                held[half].at[position[half], part],
                load_sem.at[half, part],
            )
            copy.start()
            loads.append(copy)

    def rows_of(ref):
        flat = ref[...].astype(jnp.float32)
        return jnp.concatenate([flat[:, i * width : (i + 1) * width] for i in range(pairs)], axis=0)

    q_rows, grad_rows, out_rows = rows_of(q_ref), rows_of(grad_ref), rows_of(out_ref)
    delta_column = jnp.sum(grad_rows * out_rows, axis=1, keepdims=True)
    eye = lax.broadcasted_iota(jnp.int32, (pairs, pairs), 0) == lax.broadcasted_iota(jnp.int32, (pairs, pairs), 1)
    lse_column = jnp.sum(
        jnp.where(eye, jnp.broadcast_to(lse_ref[...], (pairs, pairs)), 0.0), axis=1, keepdims=True
    )
    lane = lax.broadcasted_iota(jnp.int32, (pairs, LANES), 1)
    member = lax.rem(lax.broadcasted_iota(jnp.int32, (pairs, LANES), 0), heads)
    spot = lane == mine * heads + member
    lse_spots = jnp.where(spot, jnp.broadcast_to(lse_column, (pairs, LANES)), 0.0)
    delta_spots = jnp.where(spot, jnp.broadcast_to(delta_column, (pairs, LANES)), 0.0)
    for group in range(groups):
        rows = slice(group * heads, (group + 1) * heads)
        packet[group] = jnp.concatenate([q_rows[rows], grad_rows[rows]], axis=0).astype(jnp.bfloat16)
        packet_aux[group] = jnp.concatenate([lse_spots[rows], delta_spots[rows]], axis=0)

    pl.semaphore_wait(barrier, groups - 1 + ny - 1 + nz - 1)

    def exchange(target, origin):
        device = (target, place)
        return (
            remote(packet.at[target], got.at[origin], exchange_send.at[target, 0], exchange_recv.at[origin, 0], device),
            remote(
                packet_aux.at[target],
                got_aux.at[origin],
                exchange_send.at[target, 1],
                exchange_recv.at[origin, 1],
                device,
            ),
        )

    for d in other_coords(groups):
        for copy in exchange(lax.rem(mine + d, groups), mine):
            copy.start()
    got[mine] = packet[mine]
    got_aux[mine] = packet_aux[mine]

    def ring_parts(axis, direction, step):
        return (0, 1) if step < counts[axis] // 2 - 1 else (direction,)

    def ring_copy(axis, direction, step, part, arriving=False):
        reach = step + 1 if arriving else step
        origin = around(axis, -reach if direction == 0 else reach)
        ref = held[axis].at[origin, part]
        return remote(
            ref,
            ref,
            ring_send.at[axis, direction, step, part],
            ring_recv.at[axis, direction, step, part],
            peer(axis, around(axis, 1 if direction == 0 else -1)),
        )

    def ring_step(step):
        for part in (0, 1):
            for axis in (0, 1):
                if step >= counts[axis] // 2:
                    continue
                for direction in (0, 1):
                    if part in ring_parts(axis, direction, step):
                        if step:
                            ring_copy(axis, direction, step - 1, part, True).wait_recv()
                        ring_copy(axis, direction, step, part).start()

    for copy in loads:
        copy.wait()
    ring_step(0)

    for d in range(1, groups):
        for copy in exchange(mine, lax.rem(mine + d, groups)):
            copy.wait_recv()
    got_rows = got[...].astype(jnp.float32)
    own_block = jnp.concatenate(
        [got_rows[i, :heads] for i in range(groups)] + [got_rows[i, heads:] for i in range(groups)], axis=0
    ).astype(jnp.bfloat16)
    got_sum = jnp.sum(got_aux[...], axis=0)
    own_aux = [
        jnp.sum(got_sum[:heads], axis=0, keepdims=True),
        jnp.sum(got_sum[heads:], axis=0, keepdims=True),
    ]
    per_row = LANES // pairs
    lane_row = lax.broadcasted_iota(jnp.int32, (1, LANES), 1)

    def block_copies(half, target, origin):
        axis = 1 - half
        device = peer(axis, target)
        return (
            remote(
                block[half].at[origin],
                block[half].at[origin],
                block_send.at[half, target, 0],
                block_recv.at[half, origin, 0],
                device,
            ),
            remote(
                aux[half].at[origin],
                aux[half].at[origin],
                block_send.at[half, target, 1],
                block_recv.at[half, origin, 1],
                device,
            ),
        )

    for half in (0, 1):
        at = position[1 - half]
        block[half][at] = own_block
        inside = lax.div(lane_row, pairs) == lax.rem(at, per_row)
        spread = []
        for vector in own_aux:
            total = vector
            for k in range(1, per_row):
                total = total + pltpu.roll(vector, k * pairs, 1)
            spread.append(jnp.where(inside, total, 0.0))
        aux[half][at] = jnp.concatenate(spread, axis=0)
    for half in (0, 1):
        axis = 1 - half
        for d in reversed(other_coords(counts[axis])):
            for copy in block_copies(half, around(axis, d), position[axis]):
                copy.start()

    most = max(counts) // 2
    for step in range(1, most):
        ring_step(step)

    lse_rows, delta_rows = [], []
    for half in (0, 1):
        axis = 1 - half
        for d in other_coords(counts[axis]):
            for copy in block_copies(half, position[axis], around(axis, d)):
                copy.wait_recv()
        total_pairs = counts[axis] * pairs
        for index, found in ((0, lse_rows), (1, delta_rows)):
            pieces = []
            for first in range(0, counts[axis], per_row):
                piece = aux[half][first, index : index + 1, :]
                for j in range(first + 1, min(first + per_row, counts[axis])):
                    piece = piece + aux[half][j, index : index + 1, :]
                pieces.append(piece)
            found.append(jnp.concatenate(pieces, axis=1)[:, :total_pairs])
        turned[half][...] = jnp.zeros_like(turned[half])

    def chunk(half, index):
        total_pairs = counts[1 - half] * pairs
        q_all = block[half][:, :pairs, :].reshape(total_pairs, width)
        grad_all = block[half][:, pairs:, :].reshape(total_pairs, width)
        key, value = held[half][index, 0], held[half][index, 1]
        across = (((1,), (1,)), ((), ()))
        scores = lax.dot_general(key, q_all, across, preferred_element_type=jnp.float32)
        probs = jnp.exp(scores * scale - lse_rows[half])
        dprobs = lax.dot_general(value, grad_all, across, preferred_element_type=jnp.float32)
        dscores = (probs * (dprobs - delta_rows[half])).astype(jnp.bfloat16)
        dvalue = jnp.dot(probs.astype(jnp.bfloat16), grad_all, preferred_element_type=jnp.float32)
        dkey = jnp.dot(dscores, q_all, preferred_element_type=jnp.float32)
        turned[half][...] += lax.dot_general(
            key, dscores, (((0,), (0,)), ((), ())), preferred_element_type=jnp.float32
        )
        return dkey * scale, dvalue

    def sum_copy(axis, direction, step, part):
        return remote(
            away[axis].at[direction, step, part],
            come[axis].at[direction, step, part],
            sum_send.at[axis, direction, step, part],
            sum_recv.at[axis, direction, step, part],
            peer(axis, around(axis, 1 if direction == 0 else -1)),
        )

    def ring_target(axis, direction, step):
        reach = counts[axis] // 2 - step
        return reach if direction == 0 else counts[axis] - reach

    for half in (0, 1):
        reach = counts[half] // 2
        for direction in (0, 1):
            ring_copy(half, direction, reach - 1, direction, True).wait_recv()
        found = chunk(half, around(half, reach))
        for direction in (0, 1):
            away[half][direction, 0, direction] = found[direction].astype(jnp.bfloat16)
            sum_copy(half, direction, 0, direction).start()

    for half in (0, 1):
        reach = counts[half] // 2
        if reach > 1:
            for direction in (0, 1):
                ring_copy(half, direction, reach - 2, 1 - direction, True).wait_recv()
    for step in range(1, most):
        for half in (0, 1):
            if step < counts[half] // 2:
                for direction in (0, 1):
                    offset = ring_target(half, direction, step)
                    found = chunk(half, around(half, offset))
                    terms[half][offset, 0] = found[0]
                    terms[half][offset, 1] = found[1]
    for half in (0, 1):
        found = chunk(half, position[half])
        terms[half][0, 0] = found[0]
        terms[half][0, 1] = found[1]

    def dq_copy(half, target, origin):
        return remote(
            dq_away[half].at[target],
            dq_come[half].at[origin],
            dq_send.at[half, target],
            dq_recv.at[half, origin],
            peer(1 - half, target),
        )

    for half in (0, 1):
        axis = 1 - half
        dq_away[half][...] = jnp.transpose(turned[half][...]).reshape(counts[axis], pairs, width)
        for d in reversed(other_coords(counts[axis])):
            dq_copy(half, around(axis, d), position[axis]).start()

    def has_upstream(direction, step, part):
        return step > 1 or (step == 1 and part == direction)

    for step in range(1, most):
        for part in (0, 1):
            for half in (0, 1):
                if step >= counts[half] // 2:
                    continue
                for direction in (0, 1):
                    total = terms[half][ring_target(half, direction, step), part]
                    if has_upstream(direction, step, part):
                        sum_copy(half, direction, step - 1, part).wait_recv()
                        total = total + come[half][direction, step - 1, part].astype(jnp.float32)
                    away[half][direction, step, part] = total.astype(jnp.bfloat16)
                    sum_copy(half, direction, step, part).start()

    dq_sum = dq_away[0][position[1]] + dq_away[1][position[0]]
    for half in (0, 1):
        axis = 1 - half
        for d in other_coords(counts[axis]):
            j = around(axis, d)
            dq_copy(half, position[axis], j).wait_recv()
            dq_sum = dq_sum + dq_come[half][j]
    dq_rows = dq_sum * scale
    for group in range(groups):
        back[group] = dq_rows[group * heads : (group + 1) * heads].astype(jnp.bfloat16)

    def back_copy(target, origin):
        return remote(
            back.at[target], back_come.at[origin], back_send.at[target], back_recv.at[origin], (target, place)
        )

    for d in other_coords(groups):
        back_copy(lax.rem(mine + d, groups), mine).start()
    back_come[mine] = back[mine]

    for half in (0, 1):
        last = counts[half] // 2 - 1
        rows = pl.ds(half * half_keys, half_keys)
        for part, result in ((0, dkeys_ref), (1, dvalues_ref)):
            total = terms[half][0, part]
            for direction in (0, 1):
                if last > 0 or part == direction:
                    sum_copy(half, direction, last, part).wait_recv()
                    total = total + come[half][direction, last, part].astype(jnp.float32)
            result[rows, :] = total.astype(jnp.bfloat16)

    for d in range(1, groups):
        back_copy(mine, lax.rem(mine + d, groups)).wait_recv()
    dq_ref[...] = back_come[...]

    for d in range(1, groups):
        target = lax.rem(mine + d, groups)
        for copy in exchange(target, mine):
            copy.wait_send()
        back_copy(target, mine).wait_send()
    for half in (0, 1):
        axis = 1 - half
        for d in range(1, counts[axis]):
            target = around(axis, d)
            for copy in block_copies(half, target, position[axis]):
                copy.wait_send()
            dq_copy(half, target, position[axis]).wait_send()
        for direction in (0, 1):
            for step in range(counts[half] // 2):
                for part in ring_parts(half, direction, step):
                    ring_copy(half, direction, step, part).wait_send()
                for part in (0, 1) if step else (direction,):
                    sum_copy(half, direction, step, part).wait_send()


def shards(ny, nz, queries, out_grad, saved_out, saved_lse, video_keys, video_values):
    groups = lax.axis_size("kv")
    width = video_keys.shape[1]
    heads = queries.shape[1] // (groups * width)
    key_rows = video_keys.shape[0]
    half_keys = key_rows // 2
    pairs = groups * heads
    counts = (ny, nz)
    bf16, f32 = jnp.bfloat16, jnp.float32
    dma = pltpu.SemaphoreType.DMA
    most = max(counts)
    across = (counts[1], counts[0])
    scratch = (
        [
            pltpu.VMEM((groups, 2 * heads, width), bf16),
            pltpu.VMEM((groups, 2 * heads, LANES), f32),
            pltpu.VMEM((groups, 2 * heads, width), bf16),
            pltpu.VMEM((groups, 2 * heads, LANES), f32),
        ]
        + [pltpu.VMEM((n, 2, half_keys, width), bf16) for n in counts]
        + [pltpu.VMEM((n, 2 * pairs, width), bf16) for n in across]
        + [pltpu.VMEM((n, 2, LANES), f32) for n in across]
        + [pltpu.VMEM((n, 2, half_keys, width), f32) for n in counts]
        + [pltpu.VMEM((2, n // 2, 2, half_keys, width), bf16) for n in counts]
        + [pltpu.VMEM((2, n // 2, 2, half_keys, width), bf16) for n in counts]
        + [pltpu.VMEM((width, n * pairs), f32) for n in across]
        + [pltpu.VMEM((n, pairs, width), f32) for n in across]
        + [pltpu.VMEM((n, pairs, width), f32) for n in across]
        + [pltpu.VMEM((groups, heads, width), bf16), pltpu.VMEM((groups, heads, width), bf16)]
        + [
            dma((2, 2)),
            dma((groups, 2)),
            dma((groups, 2)),
            dma((2, 2, most // 2, 2)),
            dma((2, 2, most // 2, 2)),
            dma((2, most, 2)),
            dma((2, most, 2)),
            dma((2, 2, most // 2, 2)),
            dma((2, 2, most // 2, 2)),
            dma((2, most)),
            dma((2, most)),
            dma((groups,)),
            dma((groups,)),
        ]
    )
    vmem = pl.BlockSpec(memory_space=pltpu.VMEM)
    dq, dkeys, dvalues = pl.pallas_call(
        functools.partial(kernel, (groups, ny, nz, heads, width, half_keys)),
        out_shape=(
            jax.ShapeDtypeStruct((groups, heads, width), bf16),
            jax.ShapeDtypeStruct((key_rows, width), bf16),
            jax.ShapeDtypeStruct((key_rows, width), bf16),
        ),
        in_specs=[vmem] * 4 + [pl.BlockSpec(memory_space=pl.ANY)] * 2,
        out_specs=(vmem, vmem, vmem),
        scratch_shapes=scratch,
        compiler_params=pltpu.CompilerParams(
            collective_id=0, has_side_effects=True, vmem_limit_bytes=40 * 1024 * 1024
        ),
        name="attention_backward",
    )(queries, out_grad, saved_out, saved_lse, video_keys, video_values)
    return dq.reshape(1, groups * heads * width), dkeys, dvalues


def solution(mesh):
    seq = mesh.shape["seq"]
    ny = 1
    while ny * ny < seq:
        ny *= 2
    nz = seq // ny
    rows = P(("kv", "seq"), None)
    keys = P("seq", "kv")
    return jax.shard_map(
        functools.partial(shards, ny, nz),
        mesh=mesh,
        in_specs=(rows, rows, rows, rows, keys, keys),
        out_specs=(rows, keys, keys),
        check_vma=False,
    )
```

time: 825 us -> 58.7 us (0.07)
  waiting for transfers between devices: 703 us -> 0 us
  blocking collectives: 66.6 us -> 0 us
  Pallas kernels: 0 us -> 51.3 us
  between operations: 14 us -> 0.65 us
  matrix products: 10.7 us -> 0 us
  local copies, waits for them, and re-layouts: 17 us -> 6.35 us
  starting transfers between devices: 9.82 us -> 0 us
    unnamed x6 -> x0, waiting for transfers between devices: 447 us -> none
    all_gather x2 -> x0, waiting for transfers between devices: 254 us -> none  [the longest x1 128 us: shards(): lax.all_gather(queries, ('kv', 'seq'), axis=0, tiled=True)]
    all_gather x1 -> x0, blocking collectives: 66.6 us -> none  [shards(): lax.all_gather(saved_lse, ('kv', 'seq'), axis=0, tiled=True)]
    pallas_call x0 -> x1, Pallas kernels: none -> 51.3 us  [shards(): pl.pallas_call(functools.partial(kernel, (groups, ny, nz, heads, width, h...]
    dot_general x20 -> x0, matrix products: 10.7 us -> none  [the longest x4 6.11 us: accumulate(): jnp.einsum('nk,nd->kd', dscores, query_head, preferred_element_type=jnp.f...]
    all_to_all x1 -> x0, starting transfers between devices: 9.66 us -> none  [shards(): lax.all_to_all(rounded, 'kv', split_axis=0, concat_axis=2, tiled=True)]
  transfers between devices with their start and end apart: 5 -> 0, of which waited for: 5 -> 0; matrix products, arithmetic and copies ran while one was open for 2% -> 0% of each run, Pallas kernels for 0% -> 0%
where the time goes in v1:
time: 58.7 us; the launch traced here: 58.3 us
  Pallas kernels  51.3 us (87%)
  local copies, waits for them, and re-layouts  6.35 us (11%)
  between operations  0.65 us (1%)
    pallas_call x1, Pallas kernels, shards(): pl.pallas_call(functools.partial(kernel, (groups, ny, nz, heads, width, h...  51.3 us
    unnamed x14, local copies, waits for them, and re-layouts  5.73 us

profile of v1, /device:TPU:1, one launch (start us, length us, event | category | flops | bytes accessed | tf_op | source)
XLA Modules:
  0.0 58.3 jit_solution(1459809801933205641)
XLA Ops:
  0.6 0.0 copy-start
  0.6 0.8 %copy-done = bf16[256,128]{1,0:T(8,128)(2,1)S(1)} copy-done((bf16[256,128]{1,0:T(8,128)(2,1)S(1)}, bf16[256,128]{1,0:T(8,128)(2,1)}, u32[]{:S(2)}) %copy-start) | copy-done | bytes 65560
  1.5 0.0 copy-start.1
  1.5 0.8 %copy-done.1 = bf16[256,128]{1,0:T(8,128)(2,1)S(1)} copy-done((bf16[256,128]{1,0:T(8,128)(2,1)S(1)}, bf16[256,128]{1,0:T(8,128)(2,1)}, u32[]{:S(2)}) %copy-start.1) | copy-done | bytes 65560
  2.3 0.0 copy-start.2
  2.3 0.7 %copy-done.2 = bf16[1,4096]{1,0:T(2,128)(2,1)S(1)} copy-done((bf16[1,4096]{1,0:T(2,128)(2,1)S(1)}, bf16[1,4096]{1,0:T(2,128)(2,1)}, u32[]{:S(2)}) %copy-start.2) | copy-done | bytes 8216
  3.0 0.0 copy-start.3
  3.0 0.7 %copy-done.3 = bf16[1,4096]{1,0:T(2,128)(2,1)S(1)} copy-done((bf16[1,4096]{1,0:T(2,128)(2,1)S(1)}, bf16[1,4096]{1,0:T(2,128)(2,1)}, u32[]{:S(2)}) %copy-start.3) | copy-done | bytes 8216
  3.7 0.0 copy-start.4
  3.8 0.7 %copy-done.4 = bf16[1,4096]{1,0:T(2,128)(2,1)S(1)} copy-done((bf16[1,4096]{1,0:T(2,128)(2,1)S(1)}, bf16[1,4096]{1,0:T(2,128)(2,1)}, u32[]{:S(2)}) %copy-start.4) | copy-done | bytes 8216
  4.5 0.0 copy-start.5
  4.5 0.7 %copy-done.5 = f32[1,32]{1,0:T(1,128)S(1)} copy-done((f32[1,32]{1,0:T(1,128)S(1)}, f32[1,32]{1,0:T(1,128)}, u32[]{:S(2)}) %copy-start.5) | copy-done | bytes 152
  5.1 51.3 %attention_backward.1 = (bf16[8,4,128]{2,1,0:T(4,128)(2,1)S(1)}, bf16[256,128]{1,0:T(8,128)(2,1)S(1)}, bf16[256,128]{1,0:T(8,128)(2,1)S(1)}) custom-call(bf16[1,4096]{1,0:T(2,128)(2,1)S(1)} %copy-done.2, bf16[1,4096]{1,0:T(2,128)(2,1)S(1)} %copy-done.3, bf16[1,4096]{1,0:T(2,128)(2,1)S(1)} %copy-done.4, f32[1,32]{1,0:T(1,128)S(1)} %copy-done.5, ...), custom_call_target="tpu_custom_call" | custom-call | tf_op jit(solution)/shard_map/attention_backward/pallas_call | solution.py:444
  56.5 0.6 %reshape.9 = bf16[1,4096]{1,0:T(2,128)(2,1)} reshape(bf16[8,4,128]{2,1,0:T(4,128)(2,1)S(1)} %get-tuple-element.6) | data formatting | bytes 16384 | tf_op jit(solution)/shard_map/reshape | solution.py:459
  57.1 0.6 %copy.11 = bf16[256,128]{1,0:T(8,128)(2,1)} copy(bf16[256,128]{1,0:T(8,128)(2,1)S(1)} %get-tuple-element.13) | data formatting | bytes 131072
  57.7 0.6 %copy.12 = bf16[256,128]{1,0:T(8,128)(2,1)} copy(bf16[256,128]{1,0:T(8,128)(2,1)S(1)} %get-tuple-element.14) | data formatting | bytes 131072
Async XLA Ops:
  0.6 0.8 %copy-start = (bf16[256,128]{1,0:T(8,128)(2,1)S(1)}, bf16[256,128]{1,0:T(8,128)(2,1)}, u32[]{:S(2)}) copy-start(bf16[256,128]{1,0:T(8,128)(2,1)} %keys_ref.1) | copy-start | bytes 196612
  1.5 0.8 %copy-start.1 = (bf16[256,128]{1,0:T(8,128)(2,1)S(1)}, bf16[256,128]{1,0:T(8,128)(2,1)}, u32[]{:S(2)}) copy-start(bf16[256,128]{1,0:T(8,128)(2,1)} %values_ref.1) | copy-start | bytes 196612
  2.3 0.7 %copy-start.2 = (bf16[1,4096]{1,0:T(2,128)(2,1)S(1)}, bf16[1,4096]{1,0:T(2,128)(2,1)}, u32[]{:S(2)}) copy-start(bf16[1,4096]{1,0:T(2,128)(2,1)} %q_ref.1) | copy-start | bytes 24580
  3.0 0.7 %copy-start.3 = (bf16[1,4096]{1,0:T(2,128)(2,1)S(1)}, bf16[1,4096]{1,0:T(2,128)(2,1)}, u32[]{:S(2)}) copy-start(bf16[1,4096]{1,0:T(2,128)(2,1)} %grad_ref.1) | copy-start | bytes 24580
  3.7 0.7 %copy-start.4 = (bf16[1,4096]{1,0:T(2,128)(2,1)S(1)}, bf16[1,4096]{1,0:T(2,128)(2,1)}, u32[]{:S(2)}) copy-start(bf16[1,4096]{1,0:T(2,128)(2,1)} %out_ref.1) | copy-start | bytes 24580
  4.5 0.7 %copy-start.5 = (f32[1,32]{1,0:T(1,128)S(1)}, f32[1,32]{1,0:T(1,128)}, u32[]{:S(2)}) copy-start(f32[1,32]{1,0:T(1,128)} %lse_ref.1) | copy-start | bytes 388

commit v2 on v1

--- a/solution.py
+++ b/solution.py
@@ -18,15 +18,19 @@
 
 def kernel(
     sizes,
-    q_ref,
-    grad_ref,
-    out_ref,
-    lse_ref,
+    q_hbm,
+    grad_hbm,
+    out_hbm,
+    lse_hbm,
     keys_ref,
     values_ref,
     dq_ref,
     dkeys_ref,
     dvalues_ref,
+    q_ref,
+    grad_ref,
+    out_ref,
+    lse_ref,
     packet,
     packet_aux,
     got,
@@ -45,12 +49,15 @@
     come1,
     turned0,
     turned1,
+    dq_full0,
+    dq_full1,
     dq_away0,
     dq_away1,
     dq_come0,
     dq_come1,
     back,
     back_come,
+    row_sem,
     load_sem,
     exchange_send,
     exchange_recv,
@@ -65,11 +72,13 @@
     back_send,
     back_recv,
 ):
-    groups, ny, nz, heads, width, half_keys = sizes
+    groups, ny, nz, heads, width, half_keys, pieces = sizes
+    piece_rows = half_keys // pieces
     counts = (ny, nz)
     held, block, aux = (held0, held1), (block0, block1), (aux0, aux1)
     terms, away, come = (terms0, terms1), (away0, away1), (come0, come1)
     turned = (turned0, turned1)
+    dq_full = (dq_full0, dq_full1)
     dq_away, dq_come = (dq_away0, dq_away1), (dq_come0, dq_come1)
     pairs = groups * heads
     scale = 1.0 / math.sqrt(width)
@@ -89,6 +98,14 @@
         return pltpu.make_async_remote_copy(
             src_ref=src, dst_ref=dst, send_sem=send, recv_sem=recv, device_id=device, device_id_type=MESH
         )
+
+    row_loads = []
+    for index, (source, target) in enumerate(
+        ((q_hbm, q_ref), (grad_hbm, grad_ref), (out_hbm, out_ref), (lse_hbm, lse_ref))
+    ):
+        copy = pltpu.make_async_copy(source, target, row_sem.at[index])
+        copy.start()
+        row_loads.append(copy)
 
     barrier = pltpu.get_barrier_semaphore()
     for d in range(1, groups):
@@ -107,6 +124,9 @@
             )
             copy.start()
             loads.append(copy)
+
+    for copy in row_loads:
+        copy.wait()
 
     def rows_of(ref):
         flat = ref[...].astype(jnp.float32)
@@ -133,11 +153,11 @@
     def exchange(target, origin):
         device = (target, place)
         return (
-            remote(packet.at[target], got.at[origin], exchange_send.at[target, 0], exchange_recv.at[origin, 0], device),
+            remote(packet.at[target], got.at[origin], exchange_send.at[0], exchange_recv.at[origin, 0], device),
             remote(
                 packet_aux.at[target],
                 got_aux.at[origin],
-                exchange_send.at[target, 1],
+                exchange_send.at[0],
                 exchange_recv.at[origin, 1],
                 device,
             ),
@@ -150,22 +170,27 @@
     got_aux[mine] = packet_aux[mine]
 
     def ring_parts(axis, direction, step):
-        return (0, 1) if step < counts[axis] // 2 - 1 else (direction,)
+        kinds = (0, 1) if step < counts[axis] // 2 - 1 else (direction,)
+        return [(kind, piece) for kind in kinds for piece in range(pieces)]
+
+    every_part = [(kind, piece) for kind in (0, 1) for piece in range(pieces)]
 
     def ring_copy(axis, direction, step, part, arriving=False):
         reach = step + 1 if arriving else step
         origin = around(axis, -reach if direction == 0 else reach)
-        ref = held[axis].at[origin, part]
+        kind, piece = part
+        ref = held[axis].at[origin, kind, pl.ds(piece * piece_rows, piece_rows), :]
+        slot = kind * pieces + piece
         return remote(
             ref,
             ref,
-            ring_send.at[axis, direction, step, part],
-            ring_recv.at[axis, direction, step, part],
+            ring_send.at[0],
+            ring_recv.at[axis, direction, step, slot],
             peer(axis, around(axis, 1 if direction == 0 else -1)),
         )
 
     def ring_step(step):
-        for part in (0, 1):
+        for part in every_part:
             for axis in (0, 1):
                 if step >= counts[axis] // 2:
                     continue
@@ -175,9 +200,11 @@
                             ring_copy(axis, direction, step - 1, part, True).wait_recv()
                         ring_copy(axis, direction, step, part).start()
 
+    most = max(counts) // 2
     for copy in loads:
         copy.wait()
-    ring_step(0)
+    for step in range(min(2, most)):
+        ring_step(step)
 
     for d in range(1, groups):
         for copy in exchange(mine, lax.rem(mine + d, groups)):
@@ -201,14 +228,14 @@
             remote(
                 block[half].at[origin],
                 block[half].at[origin],
-                block_send.at[half, target, 0],
+                block_send.at[0],
                 block_recv.at[half, origin, 0],
                 device,
             ),
             remote(
                 aux[half].at[origin],
                 aux[half].at[origin],
-                block_send.at[half, target, 1],
+                block_send.at[0],
                 block_recv.at[half, origin, 1],
                 device,
             ),
@@ -231,8 +258,7 @@
             for copy in block_copies(half, around(axis, d), position[axis]):
                 copy.start()
 
-    most = max(counts) // 2
-    for step in range(1, most):
+    for step in range(2, most - 1):
         ring_step(step)
 
     lse_rows, delta_rows = [], []
@@ -243,133 +269,150 @@
                 copy.wait_recv()
         total_pairs = counts[axis] * pairs
         for index, found in ((0, lse_rows), (1, delta_rows)):
-            pieces = []
+            sums = []
             for first in range(0, counts[axis], per_row):
                 piece = aux[half][first, index : index + 1, :]
                 for j in range(first + 1, min(first + per_row, counts[axis])):
                     piece = piece + aux[half][j, index : index + 1, :]
-                pieces.append(piece)
-            found.append(jnp.concatenate(pieces, axis=1)[:, :total_pairs])
+                sums.append(piece)
+            found.append(jnp.concatenate(sums, axis=1)[:, :total_pairs])
         turned[half][...] = jnp.zeros_like(turned[half])
 
-    def chunk(half, index):
+    def chunk(half, offsets):
         total_pairs = counts[1 - half] * pairs
         q_all = block[half][:, :pairs, :].reshape(total_pairs, width)
         grad_all = block[half][:, pairs:, :].reshape(total_pairs, width)
-        key, value = held[half][index, 0], held[half][index, 1]
+        places = [around(half, offset) for offset in offsets]
+        key = jnp.concatenate([held[half][at, 0] for at in places], axis=0)
+        value = jnp.concatenate([held[half][at, 1] for at in places], axis=0)
         across = (((1,), (1,)), ((), ()))
         scores = lax.dot_general(key, q_all, across, preferred_element_type=jnp.float32)
         probs = jnp.exp(scores * scale - lse_rows[half])
         dprobs = lax.dot_general(value, grad_all, across, preferred_element_type=jnp.float32)
         dscores = (probs * (dprobs - delta_rows[half])).astype(jnp.bfloat16)
         dvalue = jnp.dot(probs.astype(jnp.bfloat16), grad_all, preferred_element_type=jnp.float32)
-        dkey = jnp.dot(dscores, q_all, preferred_element_type=jnp.float32)
+        dkey = jnp.dot(dscores, q_all, preferred_element_type=jnp.float32) * scale
         turned[half][...] += lax.dot_general(
             key, dscores, (((0,), (0,)), ((), ())), preferred_element_type=jnp.float32
         )
-        return dkey * scale, dvalue
+        for index, offset in enumerate(offsets):
+            rows = slice(index * half_keys, (index + 1) * half_keys)
+            terms[half][offset % counts[half], 0] = dkey[rows]
+            terms[half][offset % counts[half], 1] = dvalue[rows]
+
+    def sum_parts(direction, step):
+        return every_part if step else [(direction, piece) for piece in range(pieces)]
 
     def sum_copy(axis, direction, step, part):
+        kind, piece = part
+        rows = pl.ds(piece * piece_rows, piece_rows)
+        slot = kind * pieces + piece
         return remote(
-            away[axis].at[direction, step, part],
-            come[axis].at[direction, step, part],
-            sum_send.at[axis, direction, step, part],
-            sum_recv.at[axis, direction, step, part],
+            away[axis].at[direction, step, kind, rows, :],
+            come[axis].at[direction, step, kind, rows, :],
+            sum_send.at[0],
+            sum_recv.at[axis, direction, step, slot],
             peer(axis, around(axis, 1 if direction == 0 else -1)),
         )
 
-    def ring_target(axis, direction, step):
-        reach = counts[axis] // 2 - step
-        return reach if direction == 0 else counts[axis] - reach
-
+    def sum_step(step, fresh):
+        for part in every_part:
+            kind, piece = part
+            rows = pl.ds(piece * piece_rows, piece_rows)
+            for half in (0, 1):
+                reach = counts[half] // 2 - step
+                for direction in (0, 1):
+                    if reach < 1 or part not in sum_parts(direction, step):
+                        continue
+                    if fresh != (step == 0 or part not in sum_parts(direction, step - 1)):
+                        continue
+                    offset = reach if direction == 0 else counts[half] - reach
+                    total = terms[half][offset, kind, rows, :]
+                    if not fresh:
+                        sum_copy(half, direction, step - 1, part).wait_recv()
+                        total = total + come[half][direction, step - 1, kind, rows, :].astype(jnp.float32)
+                    away[half][direction, step, kind, rows, :] = total.astype(jnp.bfloat16)
+                    sum_copy(half, direction, step, part).start()
+
+    for half in (0, 1):
+        chunk(half, (0,))
+    if most > 2:
+        ring_step(most - 1)
+    for distance in range(1, most - 1):
+        for half in (0, 1):
+            if distance < counts[half] // 2 - 1:
+                chunk(half, (distance, -distance))
     for half in (0, 1):
         reach = counts[half] // 2
         for direction in (0, 1):
-            ring_copy(half, direction, reach - 1, direction, True).wait_recv()
-        found = chunk(half, around(half, reach))
-        for direction in (0, 1):
-            away[half][direction, 0, direction] = found[direction].astype(jnp.bfloat16)
-            sum_copy(half, direction, 0, direction).start()
-
+            for part in ring_parts(half, direction, reach - 1):
+                ring_copy(half, direction, reach - 1, part, True).wait_recv()
+        chunk(half, (reach,))
+    sum_step(0, True)
     for half in (0, 1):
         reach = counts[half] // 2
         if reach > 1:
             for direction in (0, 1):
-                ring_copy(half, direction, reach - 2, 1 - direction, True).wait_recv()
-    for step in range(1, most):
-        for half in (0, 1):
-            if step < counts[half] // 2:
-                for direction in (0, 1):
-                    offset = ring_target(half, direction, step)
-                    found = chunk(half, around(half, offset))
-                    terms[half][offset, 0] = found[0]
-                    terms[half][offset, 1] = found[1]
-    for half in (0, 1):
-        found = chunk(half, position[half])
-        terms[half][0, 0] = found[0]
-        terms[half][0, 1] = found[1]
+                for piece in range(pieces):
+                    ring_copy(half, direction, reach - 2, (1 - direction, piece), True).wait_recv()
+            chunk(half, (reach - 1, 1 - reach))
+    if most > 1:
+        sum_step(1, True)
 
     def dq_copy(half, target, origin):
         return remote(
             dq_away[half].at[target],
             dq_come[half].at[origin],
-            dq_send.at[half, target],
+            dq_send.at[0],
             dq_recv.at[half, origin],
             peer(1 - half, target),
         )
 
     for half in (0, 1):
         axis = 1 - half
-        dq_away[half][...] = jnp.transpose(turned[half][...]).reshape(counts[axis], pairs, width)
+        full = jnp.transpose(turned[half][...]).reshape(counts[axis], pairs, width)
+        dq_full[half][...] = full
+        dq_away[half][...] = full.astype(jnp.bfloat16)
         for d in reversed(other_coords(counts[axis])):
             dq_copy(half, around(axis, d), position[axis]).start()
 
-    def has_upstream(direction, step, part):
-        return step > 1 or (step == 1 and part == direction)
-
     for step in range(1, most):
-        for part in (0, 1):
-            for half in (0, 1):
-                if step >= counts[half] // 2:
-                    continue
-                for direction in (0, 1):
-                    total = terms[half][ring_target(half, direction, step), part]
-                    if has_upstream(direction, step, part):
-                        sum_copy(half, direction, step - 1, part).wait_recv()
-                        total = total + come[half][direction, step - 1, part].astype(jnp.float32)
-                    away[half][direction, step, part] = total.astype(jnp.bfloat16)
-                    sum_copy(half, direction, step, part).start()
-
-    dq_sum = dq_away[0][position[1]] + dq_away[1][position[0]]
+        if step > 1:
+            sum_step(step, True)
+        sum_step(step, False)
+
+    dq_sum = dq_full[0][position[1]] + dq_full[1][position[0]]
     for half in (0, 1):
         axis = 1 - half
         for d in other_coords(counts[axis]):
             j = around(axis, d)
             dq_copy(half, position[axis], j).wait_recv()
-            dq_sum = dq_sum + dq_come[half][j]
+            dq_sum = dq_sum + dq_come[half][j].astype(jnp.float32)
     dq_rows = dq_sum * scale
     for group in range(groups):
         back[group] = dq_rows[group * heads : (group + 1) * heads].astype(jnp.bfloat16)
 
     def back_copy(target, origin):
         return remote(
-            back.at[target], back_come.at[origin], back_send.at[target], back_recv.at[origin], (target, place)
+            back.at[target], back_come.at[origin], back_send.at[0], back_recv.at[origin], (target, place)
         )
 
     for d in other_coords(groups):
         back_copy(lax.rem(mine + d, groups), mine).start()
     back_come[mine] = back[mine]
 
-    for half in (0, 1):
-        last = counts[half] // 2 - 1
-        rows = pl.ds(half * half_keys, half_keys)
-        for part, result in ((0, dkeys_ref), (1, dvalues_ref)):
-            total = terms[half][0, part]
+    for part in every_part:
+        kind, piece = part
+        for half in (0, 1):
+            last = counts[half] // 2 - 1
+            rows = pl.ds(piece * piece_rows, piece_rows)
+            total = terms[half][0, kind, rows, :]
             for direction in (0, 1):
-                if last > 0 or part == direction:
+                if part in sum_parts(direction, last):
                     sum_copy(half, direction, last, part).wait_recv()
-                    total = total + come[half][direction, last, part].astype(jnp.float32)
-            result[rows, :] = total.astype(jnp.bfloat16)
+                    total = total + come[half][direction, last, kind, rows, :].astype(jnp.float32)
+            result = dvalues_ref if kind else dkeys_ref
+            result[pl.ds(half * half_keys + piece * piece_rows, piece_rows), :] = total.astype(jnp.bfloat16)
 
     for d in range(1, groups):
         back_copy(mine, lax.rem(mine + d, groups)).wait_recv()
@@ -391,8 +434,27 @@
             for step in range(counts[half] // 2):
                 for part in ring_parts(half, direction, step):
                     ring_copy(half, direction, step, part).wait_send()
-                for part in (0, 1) if step else (direction,):
+                for part in sum_parts(direction, step):
                     sum_copy(half, direction, step, part).wait_send()
+
+
+def store_kernel(dq_ref, dkeys_ref, dvalues_ref, dq_hbm, dkeys_hbm, dvalues_hbm, dq_row, sem):
+    copies = [
+        pltpu.make_async_copy(dkeys_ref, dkeys_hbm, sem.at[0]),
+        pltpu.make_async_copy(dvalues_ref, dvalues_hbm, sem.at[1]),
+        pltpu.make_async_copy(dq_row, dq_hbm, sem.at[2]),
+    ]
+    copies[0].start()
+    copies[1].start()
+    groups, heads, width = dq_ref.shape
+    for group in range(groups):
+        rows = dq_ref[group].astype(jnp.float32)
+        for head in range(heads):
+            first = (group * heads + head) * width
+            dq_row[:, first : first + width] = rows[head : head + 1].astype(jnp.bfloat16)
+    copies[2].start()
+    for copy in copies:
+        copy.wait()
 
 
 def shards(ny, nz, queries, out_grad, saved_out, saved_lse, video_keys, video_values):
@@ -407,8 +469,12 @@
     dma = pltpu.SemaphoreType.DMA
     most = max(counts)
     across = (counts[1], counts[0])
+    pieces = 2
+    row = groups * heads * width
     scratch = (
-        [
+        [pltpu.VMEM((1, row), bf16)] * 3
+        + [pltpu.VMEM((1, groups * heads), f32)]
+        + [
             pltpu.VMEM((groups, 2 * heads, width), bf16),
             pltpu.VMEM((groups, 2 * heads, LANES), f32),
             pltpu.VMEM((groups, 2 * heads, width), bf16),
@@ -422,41 +488,58 @@
         + [pltpu.VMEM((2, n // 2, 2, half_keys, width), bf16) for n in counts]
         + [pltpu.VMEM((width, n * pairs), f32) for n in across]
         + [pltpu.VMEM((n, pairs, width), f32) for n in across]
-        + [pltpu.VMEM((n, pairs, width), f32) for n in across]
+        + [pltpu.VMEM((n, pairs, width), bf16) for n in across]
+        + [pltpu.VMEM((n, pairs, width), bf16) for n in across]
         + [pltpu.VMEM((groups, heads, width), bf16), pltpu.VMEM((groups, heads, width), bf16)]
         + [
+            dma((4,)),
             dma((2, 2)),
+            dma((1,)),
             dma((groups, 2)),
-            dma((groups, 2)),
-            dma((2, 2, most // 2, 2)),
-            dma((2, 2, most // 2, 2)),
+            dma((1,)),
+            dma((2, 2, most // 2, 2 * pieces)),
+            dma((1,)),
             dma((2, most, 2)),
-            dma((2, most, 2)),
-            dma((2, 2, most // 2, 2)),
-            dma((2, 2, most // 2, 2)),
+            dma((1,)),
+            dma((2, 2, most // 2, 2 * pieces)),
+            dma((1,)),
             dma((2, most)),
-            dma((2, most)),
-            dma((groups,)),
+            dma((1,)),
             dma((groups,)),
         ]
     )
     vmem = pl.BlockSpec(memory_space=pltpu.VMEM)
+    hbm = pl.BlockSpec(memory_space=pltpu.HBM)
+    arguments = (queries, out_grad, saved_out, saved_lse, video_keys, video_values)
+    arguments = [pltpu.with_memory_space_constraint(argument, pltpu.HBM) for argument in arguments]
     dq, dkeys, dvalues = pl.pallas_call(
-        functools.partial(kernel, (groups, ny, nz, heads, width, half_keys)),
+        functools.partial(kernel, (groups, ny, nz, heads, width, half_keys, pieces)),
         out_shape=(
             jax.ShapeDtypeStruct((groups, heads, width), bf16),
             jax.ShapeDtypeStruct((key_rows, width), bf16),
             jax.ShapeDtypeStruct((key_rows, width), bf16),
         ),
-        in_specs=[vmem] * 4 + [pl.BlockSpec(memory_space=pl.ANY)] * 2,
+        in_specs=[hbm] * 6,
         out_specs=(vmem, vmem, vmem),
         scratch_shapes=scratch,
         compiler_params=pltpu.CompilerParams(
             collective_id=0, has_side_effects=True, vmem_limit_bytes=40 * 1024 * 1024
         ),
         name="attention_backward",
-    )(queries, out_grad, saved_out, saved_lse, video_keys, video_values)
-    return dq.reshape(1, groups * heads * width), dkeys, dvalues
+    )(*arguments)
+    return pl.pallas_call(
+        store_kernel,
+        out_shape=(
+            jax.ShapeDtypeStruct((1, row), bf16),
+            jax.ShapeDtypeStruct((key_rows, width), bf16),
+            jax.ShapeDtypeStruct((key_rows, width), bf16),
+        ),
+        in_specs=[vmem] * 3,
+        out_specs=(hbm, hbm, hbm),
+        scratch_shapes=[pltpu.VMEM((1, row), bf16), dma((3,))],
+        compiler_params=pltpu.CompilerParams(vmem_limit_bytes=1024 * 1024),
+        name="store_results",
+    )(dq, dkeys, dvalues)
 
 
 def solution(mesh):

time: 58.7 us -> 48.4 us (0.82)
  local copies, waits for them, and re-layouts: 6.35 us -> 0 us
  Pallas kernels: 51.3 us -> 47.6 us
    unnamed x14 -> x0, local copies, waits for them, and re-layouts: 5.73 us -> none
    pallas_call x1, Pallas kernels: 51.3 us -> 46.9 us  [shards(): pl.pallas_call(functools.partial(kernel, (groups, ny, nz, heads, width, h...]
    pallas_call x0 -> x1, Pallas kernels: none -> 0.68 us  [shards(): pl.pallas_call(store_kernel, out_shape=(jax.ShapeDtypeStruct((1, row), bf...]
    reshape x1 -> x0, local copies, waits for them, and re-layouts: 0.62 us -> none  [shards(): return (dq.reshape(1, groups * heads * width), dkeys, dvalues)]
where the time goes in v2:
time: 48.4 us; the launch traced here: 48.2 us
  Pallas kernels  47.6 us (98%)
  between operations  0.64 us (1%)
    pallas_call x1, Pallas kernels, shards(): pl.pallas_call(functools.partial(kernel, (groups, ny, nz, heads, width, h...  46.9 us

profile of v2, /device:TPU:1, one launch (start us, length us, event | category | flops | bytes accessed | tf_op | source)
XLA Modules:
  0.0 48.2 jit_solution(5444047052288443883)
XLA Ops:
  0.6 46.9 %attention_backward.1 = (bf16[8,4,128]{2,1,0:T(4,128)(2,1)S(1)}, bf16[256,128]{1,0:T(8,128)(2,1)S(1)}, bf16[256,128]{1,0:T(8,128)(2,1)S(1)}) custom-call(bf16[1,4096]{1,0:T(2,128)(2,1)} %q_hbm.1, bf16[1,4096]{1,0:T(2,128)(2,1)} %grad_hbm.1, bf16[1,4096]{1,0:T(2,128)(2,1)} %out_hbm.1, f32[1,32]{1,0:T(1,128)} %lse_hbm.1, bf16[256,128]{1,0:T(8,128)(2,1)} %keys_ref.1, ...), custom_call_target="tpu_custom_call" | custom-call | tf_op jit(solution)/shard_map/attention_backward/pallas_call | solution.py:515
  47.5 0.7 %store_results.1 = (bf16[1,4096]{1,0:T(2,128)(2,1)}, bf16[256,128]{1,0:T(8,128)(2,1)}, bf16[256,128]{1,0:T(8,128)(2,1)}) custom-call(bf16[8,4,128]{2,1,0:T(4,128)(2,1)S(1)} %get-tuple-element.6.dq_ref, bf16[256,128]{1,0:T(8,128)(2,1)S(1)} %get-tuple-element.7.dkeys_ref, bf16[256,128]{1,0:T(8,128)(2,1)S(1)} %get-tuple-element.8.dvalues_ref), custom_call_target="tpu_custom_call" | custom-call | tf_op jit(solution)/shard_map/store_results/pallas_call | solution.py:530

commit v3 on v2

--- a/solution.py
+++ b/solution.py
@@ -59,17 +59,15 @@
     back_come,
     row_sem,
     load_sem,
-    exchange_send,
+    send_sem,
     exchange_recv,
-    ring_send,
-    ring_recv,
-    block_send,
+    near_recv,
+    two_recv,
+    far_recv,
     block_recv,
-    sum_send,
-    sum_recv,
-    dq_send,
+    up_recv,
+    last_recv,
     dq_recv,
-    back_send,
     back_recv,
 ):
     groups, ny, nz, heads, width, half_keys, pieces = sizes
@@ -98,6 +96,9 @@
         return pltpu.make_async_remote_copy(
             src_ref=src, dst_ref=dst, send_sem=send, recv_sem=recv, device_id=device, device_id_type=MESH
         )
+
+    def wait_bytes(ref, sem):
+        remote(ref, ref, send_sem.at[0], sem, (lax.rem(mine + 1, groups), place)).wait_recv()
 
     row_loads = []
     for index, (source, target) in enumerate(
@@ -153,12 +154,12 @@
     def exchange(target, origin):
         device = (target, place)
         return (
-            remote(packet.at[target], got.at[origin], exchange_send.at[0], exchange_recv.at[origin, 0], device),
+            remote(packet.at[target], got.at[origin], send_sem.at[0], exchange_recv.at[0], device),
             remote(
                 packet_aux.at[target],
                 got_aux.at[origin],
-                exchange_send.at[0],
-                exchange_recv.at[origin, 1],
+                send_sem.at[0],
+                exchange_recv.at[1],
                 device,
             ),
         )
@@ -169,46 +170,54 @@
     got[mine] = packet[mine]
     got_aux[mine] = packet_aux[mine]
 
-    def ring_parts(axis, direction, step):
-        kinds = (0, 1) if step < counts[axis] // 2 - 1 else (direction,)
+    every_part = [(kind, piece) for kind in (0, 1) for piece in range(pieces)]
+    streams = [(axis, direction) for axis in (0, 1) for direction in (0, 1)]
+
+    def farthest(axis):
+        return counts[axis] // 2
+
+    def parts_at(axis, direction, distance):
+        kinds = (0, 1) if distance < farthest(axis) else (direction,)
         return [(kind, piece) for kind in kinds for piece in range(pieces)]
 
-    every_part = [(kind, piece) for kind in (0, 1) for piece in range(pieces)]
-
-    def ring_copy(axis, direction, step, part, arriving=False):
-        reach = step + 1 if arriving else step
-        origin = around(axis, -reach if direction == 0 else reach)
+    def stop(distance):
+        return 2 if distance > 2 else 0
+
+    def toward(direction, steps):
+        return steps if direction == 0 else -steps
+
+    def gather_copy(axis, direction, distance, part, arriving=False):
         kind, piece = part
-        ref = held[axis].at[origin, kind, pl.ds(piece * piece_rows, piece_rows), :]
-        slot = kind * pieces + piece
-        return remote(
-            ref,
-            ref,
-            ring_send.at[0],
-            ring_recv.at[axis, direction, step, slot],
-            peer(axis, around(axis, 1 if direction == 0 else -1)),
-        )
-
-    def ring_step(step):
-        for part in every_part:
-            for axis in (0, 1):
-                if step >= counts[axis] // 2:
-                    continue
-                for direction in (0, 1):
-                    if part in ring_parts(axis, direction, step):
-                        if step:
-                            ring_copy(axis, direction, step - 1, part, True).wait_recv()
-                        ring_copy(axis, direction, step, part).start()
-
-    most = max(counts) // 2
+        reach = distance if arriving else stop(distance)
+        ref = held[axis].at[around(axis, toward(direction, -reach)), kind, pl.ds(piece * piece_rows, piece_rows), :]
+        if distance == 1:
+            sem = near_recv.at[axis]
+        elif distance == 2:
+            sem = two_recv.at[axis, direction, kind * pieces + piece]
+        else:
+            sem = far_recv.at[axis, distance - 3]
+        target = peer(axis, around(axis, toward(direction, distance - stop(distance))))
+        return remote(ref, ref, send_sem.at[1], sem, target)
+
+    def gather_wait(axis, distance):
+        if distance == 2:
+            for direction in (0, 1):
+                for part in parts_at(axis, direction, distance):
+                    gather_copy(axis, direction, distance, part, True).wait_recv()
+        else:
+            sem = near_recv.at[axis] if distance == 1 else far_recv.at[axis, distance - 3]
+            wait_bytes(held[axis].at[pl.ds(0, 2 if distance < farthest(axis) else 1)], sem)
+
     for copy in loads:
         copy.wait()
-    for step in range(min(2, most)):
-        ring_step(step)
-
-    for d in range(1, groups):
-        for copy in exchange(mine, lax.rem(mine + d, groups)):
-            copy.wait_recv()
+    for distance in (2, 1):
+        for part in every_part:
+            for axis, direction in streams:
+                if distance <= farthest(axis) and part in parts_at(axis, direction, distance):
+                    gather_copy(axis, direction, distance, part).start()
+
+    wait_bytes(got.at[pl.ds(0, groups - 1)], exchange_recv.at[0])
+    wait_bytes(got_aux.at[pl.ds(0, groups - 1)], exchange_recv.at[1])
     got_rows = got[...].astype(jnp.float32)
     own_block = jnp.concatenate(
         [got_rows[i, :heads] for i in range(groups)] + [got_rows[i, heads:] for i in range(groups)], axis=0
@@ -228,15 +237,15 @@
             remote(
                 block[half].at[origin],
                 block[half].at[origin],
-                block_send.at[0],
-                block_recv.at[half, origin, 0],
+                send_sem.at[2],
+                block_recv.at[half, 0],
                 device,
             ),
             remote(
                 aux[half].at[origin],
                 aux[half].at[origin],
-                block_send.at[0],
-                block_recv.at[half, origin, 1],
+                send_sem.at[2],
+                block_recv.at[half, 1],
                 device,
             ),
         )
@@ -258,15 +267,19 @@
             for copy in block_copies(half, around(axis, d), position[axis]):
                 copy.start()
 
-    for step in range(2, most - 1):
-        ring_step(step)
+    for part in every_part:
+        for axis, direction in streams:
+            if farthest(axis) > 2:
+                gather_copy(axis, direction, 2, part, True).wait_recv()
+                for distance in range(3, farthest(axis) + 1):
+                    if part in parts_at(axis, direction, distance):
+                        gather_copy(axis, direction, distance, part).start()
 
     lse_rows, delta_rows = [], []
     for half in (0, 1):
         axis = 1 - half
-        for d in other_coords(counts[axis]):
-            for copy in block_copies(half, position[axis], around(axis, d)):
-                copy.wait_recv()
+        wait_bytes(block[half].at[pl.ds(0, counts[axis] - 1)], block_recv.at[half, 0])
+        wait_bytes(aux[half].at[pl.ds(0, counts[axis] - 1)], block_recv.at[half, 1])
         total_pairs = counts[axis] * pairs
         for index, found in ((0, lse_rows), (1, delta_rows)):
             sums = []
@@ -300,71 +313,66 @@
             terms[half][offset % counts[half], 0] = dkey[rows]
             terms[half][offset % counts[half], 1] = dvalue[rows]
 
-    def sum_parts(direction, step):
-        return every_part if step else [(direction, piece) for piece in range(pieces)]
-
-    def sum_copy(axis, direction, step, part):
+    def sum_copy(axis, direction, distance, part):
         kind, piece = part
         rows = pl.ds(piece * piece_rows, piece_rows)
-        slot = kind * pieces + piece
+        if distance > 2:
+            sem = up_recv.at[axis, direction, distance - 3, kind * pieces + piece]
+        else:
+            sem = last_recv.at[axis, distance - 1]
         return remote(
-            away[axis].at[direction, step, kind, rows, :],
-            come[axis].at[direction, step, kind, rows, :],
-            sum_send.at[0],
-            sum_recv.at[axis, direction, step, slot],
-            peer(axis, around(axis, 1 if direction == 0 else -1)),
-        )
-
-    def sum_step(step, fresh):
+            away[axis].at[direction, distance - 1, kind, rows, :],
+            come[axis].at[direction, distance - 1, kind, rows, :],
+            send_sem.at[3],
+            sem,
+            peer(axis, around(axis, toward(direction, distance - stop(distance)))),
+        )
+
+    def sum_send(distance, axes=(0, 1)):
         for part in every_part:
             kind, piece = part
             rows = pl.ds(piece * piece_rows, piece_rows)
-            for half in (0, 1):
-                reach = counts[half] // 2 - step
-                for direction in (0, 1):
-                    if reach < 1 or part not in sum_parts(direction, step):
-                        continue
-                    if fresh != (step == 0 or part not in sum_parts(direction, step - 1)):
-                        continue
-                    offset = reach if direction == 0 else counts[half] - reach
-                    total = terms[half][offset, kind, rows, :]
-                    if not fresh:
-                        sum_copy(half, direction, step - 1, part).wait_recv()
-                        total = total + come[half][direction, step - 1, kind, rows, :].astype(jnp.float32)
-                    away[half][direction, step, kind, rows, :] = total.astype(jnp.bfloat16)
-                    sum_copy(half, direction, step, part).start()
-
+            for axis, direction in streams:
+                if axis not in axes or distance > farthest(axis) or part not in parts_at(axis, direction, distance):
+                    continue
+                total = terms[axis][toward(direction, distance) % counts[axis], kind, rows, :]
+                if distance == 2:
+                    for beyond in range(3, farthest(axis) + 1):
+                        if part in parts_at(axis, direction, beyond):
+                            sum_copy(axis, direction, beyond, part).wait_recv()
+                            total = total + come[axis][direction, beyond - 1, kind, rows, :].astype(jnp.float32)
+                away[axis][direction, distance - 1, kind, rows, :] = total.astype(jnp.bfloat16)
+                sum_copy(axis, direction, distance, part).start()
+
+    most = max(counts) // 2
     for half in (0, 1):
         chunk(half, (0,))
-    if most > 2:
-        ring_step(most - 1)
     for distance in range(1, most - 1):
         for half in (0, 1):
-            if distance < counts[half] // 2 - 1:
+            if distance < farthest(half) - 1:
+                if distance == 1:
+                    gather_wait(half, 1)
                 chunk(half, (distance, -distance))
-    for half in (0, 1):
-        reach = counts[half] // 2
-        for direction in (0, 1):
-            for part in ring_parts(half, direction, reach - 1):
-                ring_copy(half, direction, reach - 1, part, True).wait_recv()
-        chunk(half, (reach,))
-    sum_step(0, True)
-    for half in (0, 1):
-        reach = counts[half] // 2
-        if reach > 1:
-            for direction in (0, 1):
-                for piece in range(pieces):
-                    ring_copy(half, direction, reach - 2, (1 - direction, piece), True).wait_recv()
-            chunk(half, (reach - 1, 1 - reach))
-    if most > 1:
-        sum_step(1, True)
+    sum_send(1, [axis for axis in (0, 1) if farthest(axis) > 2])
+    for half in (0, 1):
+        gather_wait(half, farthest(half))
+        chunk(half, (farthest(half),))
+    if most > 2:
+        sum_send(most)
+    for half in (0, 1):
+        before = farthest(half) - 1
+        if before > 0:
+            gather_wait(half, before)
+            chunk(half, (before, -before))
+    for distance in range(most - 1, 2, -1):
+        sum_send(distance)
 
     def dq_copy(half, target, origin):
         return remote(
             dq_away[half].at[target],
             dq_come[half].at[origin],
-            dq_send.at[0],
-            dq_recv.at[half, origin],
+            send_sem.at[4],
+            dq_recv.at[half],
             peer(1 - half, target),
         )
 
@@ -376,46 +384,44 @@
         for d in reversed(other_coords(counts[axis])):
             dq_copy(half, around(axis, d), position[axis]).start()
 
-    for step in range(1, most):
-        if step > 1:
-            sum_step(step, True)
-        sum_step(step, False)
-
+    sum_send(1, [axis for axis in (0, 1) if farthest(axis) <= 2])
+    sum_send(2)
+
+    for half in (0, 1):
+        axis = 1 - half
+        wait_bytes(dq_come[half].at[pl.ds(0, counts[axis] - 1)], dq_recv.at[half])
     dq_sum = dq_full[0][position[1]] + dq_full[1][position[0]]
     for half in (0, 1):
         axis = 1 - half
-        for d in other_coords(counts[axis]):
-            j = around(axis, d)
-            dq_copy(half, position[axis], j).wait_recv()
-            dq_sum = dq_sum + dq_come[half][j].astype(jnp.float32)
+        for d in range(1, counts[axis]):
+            dq_sum = dq_sum + dq_come[half][around(axis, d)].astype(jnp.float32)
     dq_rows = dq_sum * scale
     for group in range(groups):
         back[group] = dq_rows[group * heads : (group + 1) * heads].astype(jnp.bfloat16)
 
     def back_copy(target, origin):
         return remote(
-            back.at[target], back_come.at[origin], back_send.at[0], back_recv.at[origin], (target, place)
+            back.at[target], back_come.at[origin], send_sem.at[5], back_recv.at[0], (target, place)
         )
 
     for d in other_coords(groups):
         back_copy(lax.rem(mine + d, groups), mine).start()
     back_come[mine] = back[mine]
 
-    for part in every_part:
-        kind, piece = part
-        for half in (0, 1):
-            last = counts[half] // 2 - 1
-            rows = pl.ds(piece * piece_rows, piece_rows)
-            total = terms[half][0, kind, rows, :]
+    for axis in (0, 1):
+        for distance in range(1, min(2, farthest(axis)) + 1):
+            whole = come[axis].at[:, distance - 1] if distance < farthest(axis) else come[axis].at[0, distance - 1]
+            wait_bytes(whole, last_recv.at[axis, distance - 1])
+    for half in (0, 1):
+        for kind, result in ((0, dkeys_ref), (1, dvalues_ref)):
+            total = terms[half][0, kind]
             for direction in (0, 1):
-                if part in sum_parts(direction, last):
-                    sum_copy(half, direction, last, part).wait_recv()
-                    total = total + come[half][direction, last, kind, rows, :].astype(jnp.float32)
-            result = dvalues_ref if kind else dkeys_ref
-            result[pl.ds(half * half_keys + piece * piece_rows, piece_rows), :] = total.astype(jnp.bfloat16)
-
-    for d in range(1, groups):
-        back_copy(mine, lax.rem(mine + d, groups)).wait_recv()
+                for distance in (1, 2):
+                    if distance <= farthest(half) and (kind, 0) in parts_at(half, direction, distance):
+                        total = total + come[half][direction, distance - 1, kind].astype(jnp.float32)
+            result[pl.ds(half * half_keys, half_keys), :] = total.astype(jnp.bfloat16)
+
+    wait_bytes(back_come.at[pl.ds(0, groups - 1)], back_recv.at[0])
     dq_ref[...] = back_come[...]
 
     for d in range(1, groups):
@@ -431,11 +437,10 @@
                 copy.wait_send()
             dq_copy(half, target, position[axis]).wait_send()
         for direction in (0, 1):
-            for step in range(counts[half] // 2):
-                for part in ring_parts(half, direction, step):
-                    ring_copy(half, direction, step, part).wait_send()
-                for part in sum_parts(direction, step):
-                    sum_copy(half, direction, step, part).wait_send()
+            for distance in range(1, farthest(half) + 1):
+                for part in parts_at(half, direction, distance):
+                    gather_copy(half, direction, distance, part).wait_send()
+                    sum_copy(half, direction, distance, part).wait_send()
 
 
 def store_kernel(dq_ref, dkeys_ref, dvalues_ref, dq_hbm, dkeys_hbm, dvalues_hbm, dq_row, sem):
@@ -467,7 +472,6 @@
     counts = (ny, nz)
     bf16, f32 = jnp.bfloat16, jnp.float32
     dma = pltpu.SemaphoreType.DMA
-    most = max(counts)
     across = (counts[1], counts[0])
     pieces = 2
     row = groups * heads * width
@@ -494,18 +498,16 @@
         + [
             dma((4,)),
             dma((2, 2)),
+            dma((6,)),
+            dma((2,)),
+            dma((2,)),
+            dma((2, 2, 2 * pieces)),
+            dma((2, 2)),
+            dma((2, 2)),
+            dma((2, 2, 2, 2 * pieces)),
+            dma((2, 2)),
+            dma((2,)),
             dma((1,)),
-            dma((groups, 2)),
-            dma((1,)),
-            dma((2, 2, most // 2, 2 * pieces)),
-            dma((1,)),
-            dma((2, most, 2)),
-            dma((1,)),
-            dma((2, 2, most // 2, 2 * pieces)),
-            dma((1,)),
-            dma((2, most)),
-            dma((1,)),
-            dma((groups,)),
         ]
     )
     vmem = pl.BlockSpec(memory_space=pltpu.VMEM)

time: 48.4 us -> 41.9 us (0.87)
  Pallas kernels: 47.6 us -> 41.1 us
    pallas_call x1, Pallas kernels: 46.9 us -> 40.4 us  [shards(): pl.pallas_call(functools.partial(kernel, (groups, ny, nz, heads, width, h...]
where the time goes in v3:
time: 41.9 us; the launch traced here: 41.7 us
  Pallas kernels  41.1 us (98%)
  between operations  0.64 us (2%)
    pallas_call x1, Pallas kernels, shards(): pl.pallas_call(functools.partial(kernel, (groups, ny, nz, heads, width, h...  40.4 us

profile of v3, /device:TPU:1, one launch (start us, length us, event | category | flops | bytes accessed | tf_op | source)
XLA Modules:
  0.0 41.7 jit_solution(13703317222953320898)
XLA Ops:
  0.6 40.4 %attention_backward.1 = (bf16[8,4,128]{2,1,0:T(4,128)(2,1)S(1)}, bf16[256,128]{1,0:T(8,128)(2,1)S(1)}, bf16[256,128]{1,0:T(8,128)(2,1)S(1)}) custom-call(bf16[1,4096]{1,0:T(2,128)(2,1)} %q_hbm.1, bf16[1,4096]{1,0:T(2,128)(2,1)} %grad_hbm.1, bf16[1,4096]{1,0:T(2,128)(2,1)} %out_hbm.1, f32[1,32]{1,0:T(1,128)} %lse_hbm.1, bf16[256,128]{1,0:T(8,128)(2,1)} %keys_ref.1, ...), custom_call_target="tpu_custom_call" | custom-call | tf_op jit(solution)/shard_map/attention_backward/pallas_call | solution.py:517
  41.1 0.7 %store_results.1 = (bf16[1,4096]{1,0:T(2,128)(2,1)}, bf16[256,128]{1,0:T(8,128)(2,1)}, bf16[256,128]{1,0:T(8,128)(2,1)}) custom-call(bf16[8,4,128]{2,1,0:T(4,128)(2,1)S(1)} %get-tuple-element.6.dq_ref, bf16[256,128]{1,0:T(8,128)(2,1)S(1)} %get-tuple-element.7.dkeys_ref, bf16[256,128]{1,0:T(8,128)(2,1)S(1)} %get-tuple-element.8.dvalues_ref), custom_call_target="tpu_custom_call" | custom-call | tf_op jit(solution)/shard_map/store_results/pallas_call | solution.py:532

commit v4 on v3

--- a/solution.py
+++ b/solution.py
@@ -14,6 +14,10 @@
 
 def other_coords(count):
     return sorted(range(1, count), key=lambda d: (min(d, count - d), d))
+
+
+def near_offsets(count):
+    return [d for d in range(1, count) if min(d, count - d) <= 2]
 
 
 def kernel(
@@ -56,9 +60,9 @@
     dq_come0,
     dq_come1,
     back,
-    back_come,
     row_sem,
     load_sem,
+    entered,
     send_sem,
     exchange_recv,
     near_recv,
@@ -112,7 +116,7 @@
     for d in range(1, groups):
         pl.semaphore_signal(barrier, inc=1, device_id=(lax.rem(mine + d, groups), place), device_id_type=MESH)
     for axis in (0, 1):
-        for d in range(1, counts[axis]):
+        for d in near_offsets(counts[axis]):
             pl.semaphore_signal(barrier, inc=1, device_id=peer(axis, around(axis, d)), device_id_type=MESH)
 
     loads = []
@@ -149,7 +153,13 @@
         packet[group] = jnp.concatenate([q_rows[rows], grad_rows[rows]], axis=0).astype(jnp.bfloat16)
         packet_aux[group] = jnp.concatenate([lse_spots[rows], delta_spots[rows]], axis=0)
 
-    pl.semaphore_wait(barrier, groups - 1 + ny - 1 + nz - 1)
+    pl.semaphore_wait(barrier, groups - 1 + len(near_offsets(ny)) + len(near_offsets(nz)))
+    relayed = 0
+    for axis in (0, 1):
+        if counts[axis] > 5:
+            relayed += 2
+            for d in (2, -2):
+                pl.semaphore_signal(entered, inc=1, device_id=peer(axis, around(axis, d)), device_id_type=MESH)
 
     def exchange(target, origin):
         device = (target, place)
@@ -218,6 +228,8 @@
 
     wait_bytes(got.at[pl.ds(0, groups - 1)], exchange_recv.at[0])
     wait_bytes(got_aux.at[pl.ds(0, groups - 1)], exchange_recv.at[1])
+    if relayed:
+        pl.semaphore_wait(entered, relayed)
     got_rows = got[...].astype(jnp.float32)
     own_block = jnp.concatenate(
         [got_rows[i, :heads] for i in range(groups)] + [got_rows[i, heads:] for i in range(groups)], axis=0
@@ -291,27 +303,32 @@
             found.append(jnp.concatenate(sums, axis=1)[:, :total_pairs])
         turned[half][...] = jnp.zeros_like(turned[half])
 
-    def chunk(half, offsets):
-        total_pairs = counts[1 - half] * pairs
-        q_all = block[half][:, :pairs, :].reshape(total_pairs, width)
-        grad_all = block[half][:, pairs:, :].reshape(total_pairs, width)
-        places = [around(half, offset) for offset in offsets]
-        key = jnp.concatenate([held[half][at, 0] for at in places], axis=0)
-        value = jnp.concatenate([held[half][at, 1] for at in places], axis=0)
-        across = (((1,), (1,)), ((), ()))
-        scores = lax.dot_general(key, q_all, across, preferred_element_type=jnp.float32)
-        probs = jnp.exp(scores * scale - lse_rows[half])
-        dprobs = lax.dot_general(value, grad_all, across, preferred_element_type=jnp.float32)
-        dscores = (probs * (dprobs - delta_rows[half])).astype(jnp.bfloat16)
-        dvalue = jnp.dot(probs.astype(jnp.bfloat16), grad_all, preferred_element_type=jnp.float32)
-        dkey = jnp.dot(dscores, q_all, preferred_element_type=jnp.float32) * scale
-        turned[half][...] += lax.dot_general(
-            key, dscores, (((0,), (0,)), ((), ())), preferred_element_type=jnp.float32
-        )
-        for index, offset in enumerate(offsets):
-            rows = slice(index * half_keys, (index + 1) * half_keys)
-            terms[half][offset % counts[half], 0] = dkey[rows]
-            terms[half][offset % counts[half], 1] = dvalue[rows]
+    def chunks(work):
+        across, down = (((1,), (1,)), ((), ())), (((0,), (0,)), ((), ()))
+        staged = []
+        for half, offsets in work:
+            total_pairs = counts[1 - half] * pairs
+            q_all = block[half][:, :pairs, :].reshape(total_pairs, width)
+            grad_all = block[half][:, pairs:, :].reshape(total_pairs, width)
+            places = [around(half, offset) for offset in offsets]
+            key = jnp.concatenate([held[half][at, 0] for at in places], axis=0)
+            value = jnp.concatenate([held[half][at, 1] for at in places], axis=0)
+            scores = lax.dot_general(key, q_all, across, preferred_element_type=jnp.float32)
+            dprobs = lax.dot_general(value, grad_all, across, preferred_element_type=jnp.float32)
+            staged.append((key, q_all, grad_all, scores, dprobs))
+        rounded = []
+        for (half, _), (_, _, _, scores, dprobs) in zip(work, staged):
+            probs = jnp.exp(scores * scale - lse_rows[half])
+            dscores = (probs * (dprobs - delta_rows[half])).astype(jnp.bfloat16)
+            rounded.append((probs.astype(jnp.bfloat16), dscores))
+        for (half, offsets), (key, q_all, grad_all, _, _), (probs, dscores) in zip(work, staged, rounded):
+            dvalue = jnp.dot(probs, grad_all, preferred_element_type=jnp.float32)
+            dkey = jnp.dot(dscores, q_all, preferred_element_type=jnp.float32) * scale
+            turned[half][...] += lax.dot_general(key, dscores, down, preferred_element_type=jnp.float32)
+            for index, offset in enumerate(offsets):
+                rows = slice(index * half_keys, (index + 1) * half_keys)
+                terms[half][offset % counts[half], 0] = dkey[rows]
+                terms[half][offset % counts[half], 1] = dvalue[rows]
 
     def sum_copy(axis, direction, distance, part):
         kind, piece = part
@@ -345,68 +362,71 @@
                 sum_copy(axis, direction, distance, part).start()
 
     most = max(counts) // 2
-    for half in (0, 1):
-        chunk(half, (0,))
-    for distance in range(1, most - 1):
-        for half in (0, 1):
-            if distance < farthest(half) - 1:
-                if distance == 1:
-                    gather_wait(half, 1)
-                chunk(half, (distance, -distance))
-    sum_send(1, [axis for axis in (0, 1) if farthest(axis) > 2])
+    long_axes = [axis for axis in (0, 1) if farthest(axis) > 2]
+    for half in long_axes:
+        gather_wait(half, 1)
+    chunks([(half, (1, -1)) for half in long_axes])
+    sum_send(1, long_axes)
+    chunks([(half, (0, 2, -2) if farthest(half) > 3 else (0,)) for half in (0, 1)])
     for half in (0, 1):
         gather_wait(half, farthest(half))
-        chunk(half, (farthest(half),))
+    chunks([(half, (farthest(half),)) for half in (0, 1)])
     if most > 2:
         sum_send(most)
-    for half in (0, 1):
-        before = farthest(half) - 1
-        if before > 0:
-            gather_wait(half, before)
-            chunk(half, (before, -before))
+    before = [(half, (farthest(half) - 1, 1 - farthest(half))) for half in (0, 1) if farthest(half) > 1]
+    for half, offsets in before:
+        gather_wait(half, offsets[0])
+    chunks(before)
     for distance in range(most - 1, 2, -1):
         sum_send(distance)
 
-    def dq_copy(half, target, origin):
+    def dq_copy(half, index, group):
+        axis = 1 - half
         return remote(
-            dq_away[half].at[target],
-            dq_come[half].at[origin],
+            dq_away[half].at[index, group],
+            dq_come[half].at[position[axis], mine],
             send_sem.at[4],
             dq_recv.at[half],
-            peer(1 - half, target),
+            (group, peer(axis, index)[1]),
         )
 
     for half in (0, 1):
         axis = 1 - half
-        full = jnp.transpose(turned[half][...]).reshape(counts[axis], pairs, width)
-        dq_full[half][...] = full
-        dq_away[half][...] = full.astype(jnp.bfloat16)
+        full = jnp.transpose(turned[half][...])
+        dq_full[half][...] = full.reshape(counts[axis], pairs, width)
+        for index in range(counts[axis]):
+            for group in range(groups):
+                first = index * pairs + group * heads
+                dq_away[half][index, group] = full[first : first + heads].astype(jnp.bfloat16)
         for d in reversed(other_coords(counts[axis])):
-            dq_copy(half, around(axis, d), position[axis]).start()
-
-    sum_send(1, [axis for axis in (0, 1) if farthest(axis) <= 2])
+            for group in range(groups):
+                dq_copy(half, around(axis, d), group).start()
+
+    def back_copy(group):
+        return remote(
+            back.at[group], dq_come[0].at[position[1], mine], send_sem.at[5], back_recv.at[0], (group, place)
+        )
+
+    own_terms = dq_full[0][position[1]] + dq_full[1][position[0]]
+    for group in range(groups):
+        back[group] = own_terms[group * heads : (group + 1) * heads].astype(jnp.bfloat16)
+    for d in other_coords(groups):
+        back_copy(lax.rem(mine + d, groups)).start()
+    dq_come[0][position[1], mine] = back[mine]
+
+    sum_send(1, [axis for axis in (0, 1) if axis not in long_axes])
     sum_send(2)
 
     for half in (0, 1):
         axis = 1 - half
         wait_bytes(dq_come[half].at[pl.ds(0, counts[axis] - 1)], dq_recv.at[half])
-    dq_sum = dq_full[0][position[1]] + dq_full[1][position[0]]
+    wait_bytes(dq_come[0].at[0, pl.ds(0, groups - 1)], back_recv.at[0])
+    dq_sum = dq_come[0][position[1]].astype(jnp.float32)
     for half in (0, 1):
         axis = 1 - half
         for d in range(1, counts[axis]):
             dq_sum = dq_sum + dq_come[half][around(axis, d)].astype(jnp.float32)
-    dq_rows = dq_sum * scale
-    for group in range(groups):
-        back[group] = dq_rows[group * heads : (group + 1) * heads].astype(jnp.bfloat16)
-
-    def back_copy(target, origin):
-        return remote(
-            back.at[target], back_come.at[origin], send_sem.at[5], back_recv.at[0], (target, place)
-        )
-
-    for d in other_coords(groups):
-        back_copy(lax.rem(mine + d, groups), mine).start()
-    back_come[mine] = back[mine]
+    dq_ref[...] = (dq_sum * scale).astype(jnp.bfloat16)
 
     for axis in (0, 1):
         for distance in range(1, min(2, farthest(axis)) + 1):
@@ -421,21 +441,19 @@
                         total = total + come[half][direction, distance - 1, kind].astype(jnp.float32)
             result[pl.ds(half * half_keys, half_keys), :] = total.astype(jnp.bfloat16)
 
-    wait_bytes(back_come.at[pl.ds(0, groups - 1)], back_recv.at[0])
-    dq_ref[...] = back_come[...]
-
     for d in range(1, groups):
         target = lax.rem(mine + d, groups)
         for copy in exchange(target, mine):
             copy.wait_send()
-        back_copy(target, mine).wait_send()
-    for half in (0, 1):
-        axis = 1 - half
+        back_copy(target).wait_send()
+    for half in (0, 1):
+        axis = 1 - half
+        sent = dq_away[half].at[pl.ds(0, counts[axis] - 1)]
+        remote(sent, sent, send_sem.at[4], dq_recv.at[half], (lax.rem(mine + 1, groups), place)).wait_send()
         for d in range(1, counts[axis]):
             target = around(axis, d)
             for copy in block_copies(half, target, position[axis]):
                 copy.wait_send()
-            dq_copy(half, target, position[axis]).wait_send()
         for direction in (0, 1):
             for distance in range(1, farthest(half) + 1):
                 for part in parts_at(half, direction, distance):
@@ -492,12 +510,13 @@
         + [pltpu.VMEM((2, n // 2, 2, half_keys, width), bf16) for n in counts]
         + [pltpu.VMEM((width, n * pairs), f32) for n in across]
         + [pltpu.VMEM((n, pairs, width), f32) for n in across]
-        + [pltpu.VMEM((n, pairs, width), bf16) for n in across]
-        + [pltpu.VMEM((n, pairs, width), bf16) for n in across]
-        + [pltpu.VMEM((groups, heads, width), bf16), pltpu.VMEM((groups, heads, width), bf16)]
+        + [pltpu.VMEM((n, groups, heads, width), bf16) for n in across]
+        + [pltpu.VMEM((n, groups, heads, width), bf16) for n in across]
+        + [pltpu.VMEM((groups, heads, width), bf16)]
         + [
             dma((4,)),
             dma((2, 2)),
+            pltpu.SemaphoreType.REGULAR,
             dma((6,)),
             dma((2,)),
             dma((2,)),

time: 41.9 us -> 39.2 us (0.936)
  Pallas kernels: 41.1 us -> 38.3 us
    pallas_call x1, Pallas kernels: 40.4 us -> 37.6 us  [shards(): pl.pallas_call(functools.partial(kernel, (groups, ny, nz, heads, width, h...]
where the time goes in v4:
time: 39.2 us; the launch traced here: 39 us
  Pallas kernels  38.3 us (98%)
  between operations  0.64 us (2%)
    pallas_call x1, Pallas kernels, shards(): pl.pallas_call(functools.partial(kernel, (groups, ny, nz, heads, width, h...  37.6 us

profile of v4, /device:TPU:1, one launch (start us, length us, event | category | flops | bytes accessed | tf_op | source)
XLA Modules:
  0.0 39.0 jit_solution(3015994129421509369)
XLA Ops:
  0.6 37.6 %attention_backward.1 = (bf16[8,4,128]{2,1,0:T(4,128)(2,1)S(1)}, bf16[256,128]{1,0:T(8,128)(2,1)S(1)}, bf16[256,128]{1,0:T(8,128)(2,1)S(1)}) custom-call(bf16[1,4096]{1,0:T(2,128)(2,1)} %q_hbm.1, bf16[1,4096]{1,0:T(2,128)(2,1)} %grad_hbm.1, bf16[1,4096]{1,0:T(2,128)(2,1)} %out_hbm.1, f32[1,32]{1,0:T(1,128)} %lse_hbm.1, bf16[256,128]{1,0:T(8,128)(2,1)} %keys_ref.1, ...), custom_call_target="tpu_custom_call" | custom-call | tf_op jit(solution)/shard_map/attention_backward/pallas_call | solution.py:536
  38.3 0.7 %store_results.1 = (bf16[1,4096]{1,0:T(2,128)(2,1)}, bf16[256,128]{1,0:T(8,128)(2,1)}, bf16[256,128]{1,0:T(8,128)(2,1)}) custom-call(bf16[8,4,128]{2,1,0:T(4,128)(2,1)S(1)} %get-tuple-element.6.dq_ref, bf16[256,128]{1,0:T(8,128)(2,1)S(1)} %get-tuple-element.7.dkeys_ref, bf16[256,128]{1,0:T(8,128)(2,1)S(1)} %get-tuple-element.8.dvalues_ref), custom_call_target="tpu_custom_call" | custom-call | tf_op jit(solution)/shard_map/store_results/pallas_call | solution.py:551

commit v5 on v4

--- a/solution.py
+++ b/solution.py
@@ -119,16 +119,13 @@
         for d in near_offsets(counts[axis]):
             pl.semaphore_signal(barrier, inc=1, device_id=peer(axis, around(axis, d)), device_id_type=MESH)
 
-    loads = []
     for half in (0, 1):
         for part, source in ((0, keys_ref), (1, values_ref)):
-            copy = pltpu.make_async_copy(
+            pltpu.make_async_copy(
                 source.at[pl.ds(half * half_keys, half_keys), :],
                 held[half].at[position[half], part],
-                load_sem.at[half, part],
-            )
-            copy.start()
-            loads.append(copy)
+                load_sem.at[0],
+            ).start()
 
     for copy in row_loads:
         copy.wait()
@@ -151,7 +148,9 @@
     for group in range(groups):
         rows = slice(group * heads, (group + 1) * heads)
         packet[group] = jnp.concatenate([q_rows[rows], grad_rows[rows]], axis=0).astype(jnp.bfloat16)
-        packet_aux[group] = jnp.concatenate([lse_spots[rows], delta_spots[rows]], axis=0)
+        packet_aux[group] = jnp.concatenate(
+            [jnp.sum(spots[rows], axis=0, keepdims=True) for spots in (lse_spots, delta_spots)], axis=0
+        )
 
     pl.semaphore_wait(barrier, groups - 1 + len(near_offsets(ny)) + len(near_offsets(nz)))
     relayed = 0
@@ -203,11 +202,11 @@
         if distance == 1:
             sem = near_recv.at[axis]
         elif distance == 2:
-            sem = two_recv.at[axis, direction, kind * pieces + piece]
+            sem = two_recv.at[axis, kind * pieces + piece]
         else:
             sem = far_recv.at[axis, distance - 3]
         target = peer(axis, around(axis, toward(direction, distance - stop(distance))))
-        return remote(ref, ref, send_sem.at[1], sem, target)
+        return remote(ref, ref, send_sem.at[0], sem, target)
 
     def gather_wait(axis, distance):
         if distance == 2:
@@ -218,8 +217,8 @@
             sem = near_recv.at[axis] if distance == 1 else far_recv.at[axis, distance - 3]
             wait_bytes(held[axis].at[pl.ds(0, 2 if distance < farthest(axis) else 1)], sem)
 
-    for copy in loads:
-        copy.wait()
+    loaded = held0.at[pl.ds(0, 2)]
+    pltpu.make_async_copy(loaded, loaded, load_sem.at[0]).wait()
     for distance in (2, 1):
         for part in every_part:
             for axis, direction in streams:
@@ -235,10 +234,7 @@
         [got_rows[i, :heads] for i in range(groups)] + [got_rows[i, heads:] for i in range(groups)], axis=0
     ).astype(jnp.bfloat16)
     got_sum = jnp.sum(got_aux[...], axis=0)
-    own_aux = [
-        jnp.sum(got_sum[:heads], axis=0, keepdims=True),
-        jnp.sum(got_sum[heads:], axis=0, keepdims=True),
-    ]
+    own_aux = [got_sum[:1], got_sum[1:]]
     per_row = LANES // pairs
     lane_row = lax.broadcasted_iota(jnp.int32, (1, LANES), 1)
 
@@ -249,14 +245,14 @@
             remote(
                 block[half].at[origin],
                 block[half].at[origin],
-                send_sem.at[2],
+                send_sem.at[0],
                 block_recv.at[half, 0],
                 device,
             ),
             remote(
                 aux[half].at[origin],
                 aux[half].at[origin],
-                send_sem.at[2],
+                send_sem.at[0],
                 block_recv.at[half, 1],
                 device,
             ),
@@ -282,7 +278,10 @@
     for part in every_part:
         for axis, direction in streams:
             if farthest(axis) > 2:
-                gather_copy(axis, direction, 2, part, True).wait_recv()
+                if direction == 0:
+                    kind, piece = part
+                    both = held[axis].at[pl.ds(0, 2), kind, pl.ds(piece * piece_rows, piece_rows), :]
+                    wait_bytes(both, two_recv.at[axis, kind * pieces + piece])
                 for distance in range(3, farthest(axis) + 1):
                     if part in parts_at(axis, direction, distance):
                         gather_copy(axis, direction, distance, part).start()
@@ -334,13 +333,13 @@
         kind, piece = part
         rows = pl.ds(piece * piece_rows, piece_rows)
         if distance > 2:
-            sem = up_recv.at[axis, direction, distance - 3, kind * pieces + piece]
+            sem = up_recv.at[axis, direction, kind * pieces + piece]
         else:
             sem = last_recv.at[axis, distance - 1]
         return remote(
             away[axis].at[direction, distance - 1, kind, rows, :],
             come[axis].at[direction, distance - 1, kind, rows, :],
-            send_sem.at[3],
+            send_sem.at[0],
             sem,
             peer(axis, around(axis, toward(direction, distance - stop(distance)))),
         )
@@ -354,10 +353,12 @@
                     continue
                 total = terms[axis][toward(direction, distance) % counts[axis], kind, rows, :]
                 if distance == 2:
-                    for beyond in range(3, farthest(axis) + 1):
-                        if part in parts_at(axis, direction, beyond):
-                            sum_copy(axis, direction, beyond, part).wait_recv()
-                            total = total + come[axis][direction, beyond - 1, kind, rows, :].astype(jnp.float32)
+                    beyonds = [d for d in range(3, farthest(axis) + 1) if part in parts_at(axis, direction, d)]
+                    if beyonds:
+                        arrived = come[axis].at[direction, pl.ds(2, len(beyonds)), kind, rows, :]
+                        wait_bytes(arrived, up_recv.at[axis, direction, kind * pieces + piece])
+                    for beyond in beyonds:
+                        total = total + come[axis][direction, beyond - 1, kind, rows, :].astype(jnp.float32)
                 away[axis][direction, distance - 1, kind, rows, :] = total.astype(jnp.bfloat16)
                 sum_copy(axis, direction, distance, part).start()
 
@@ -385,7 +386,7 @@
         return remote(
             dq_away[half].at[index, group],
             dq_come[half].at[position[axis], mine],
-            send_sem.at[4],
+            send_sem.at[0],
             dq_recv.at[half],
             (group, peer(axis, index)[1]),
         )
@@ -404,7 +405,7 @@
 
     def back_copy(group):
         return remote(
-            back.at[group], dq_come[0].at[position[1], mine], send_sem.at[5], back_recv.at[0], (group, place)
+            back.at[group], dq_come[0].at[position[1], mine], send_sem.at[0], back_recv.at[0], (group, place)
         )
 
     own_terms = dq_full[0][position[1]] + dq_full[1][position[0]]
@@ -449,7 +450,7 @@
     for half in (0, 1):
         axis = 1 - half
         sent = dq_away[half].at[pl.ds(0, counts[axis] - 1)]
-        remote(sent, sent, send_sem.at[4], dq_recv.at[half], (lax.rem(mine + 1, groups), place)).wait_send()
+        remote(sent, sent, send_sem.at[0], dq_recv.at[half], (lax.rem(mine + 1, groups), place)).wait_send()
         for d in range(1, counts[axis]):
             target = around(axis, d)
             for copy in block_copies(half, target, position[axis]):
@@ -498,9 +499,9 @@
         + [pltpu.VMEM((1, groups * heads), f32)]
         + [
             pltpu.VMEM((groups, 2 * heads, width), bf16),
-            pltpu.VMEM((groups, 2 * heads, LANES), f32),
+            pltpu.VMEM((groups, 2, LANES), f32),
             pltpu.VMEM((groups, 2 * heads, width), bf16),
-            pltpu.VMEM((groups, 2 * heads, LANES), f32),
+            pltpu.VMEM((groups, 2, LANES), f32),
         ]
         + [pltpu.VMEM((n, 2, half_keys, width), bf16) for n in counts]
         + [pltpu.VMEM((n, 2 * pairs, width), bf16) for n in across]
@@ -515,15 +516,15 @@
         + [pltpu.VMEM((groups, heads, width), bf16)]
         + [
             dma((4,)),
-            dma((2, 2)),
+            dma((1,)),
             pltpu.SemaphoreType.REGULAR,
-            dma((6,)),
+            dma((1,)),
             dma((2,)),
             dma((2,)),
-            dma((2, 2, 2 * pieces)),
+            dma((2, 2 * pieces)),
             dma((2, 2)),
             dma((2, 2)),
-            dma((2, 2, 2, 2 * pieces)),
+            dma((2, 2, 2 * pieces)),
             dma((2, 2)),
             dma((2,)),
             dma((1,)),

time: 39.2 us -> 38.9 us (level); the launches traced: 39 us -> 38.2 us
  Pallas kernels: 38.3 us -> 37.6 us
    pallas_call x1, Pallas kernels: 37.6 us -> 36.9 us  [shards(): pl.pallas_call(functools.partial(kernel, (groups, ny, nz, heads, width, h...]
where the time goes in v5:
time: 38.9 us; the launch traced here: 38.2 us
  Pallas kernels  37.6 us (97%)
  between operations  0.64 us (2%)
    pallas_call x1, Pallas kernels, shards(): pl.pallas_call(functools.partial(kernel, (groups, ny, nz, heads, width, h...  36.9 us

profile of v5, /device:TPU:1, one launch (start us, length us, event | category | flops | bytes accessed | tf_op | source)
XLA Modules:
  0.0 38.2 jit_solution(16727466404162209372)
XLA Ops:
  0.6 36.9 %attention_backward.1 = (bf16[8,4,128]{2,1,0:T(4,128)(2,1)S(1)}, bf16[256,128]{1,0:T(8,128)(2,1)S(1)}, bf16[256,128]{1,0:T(8,128)(2,1)S(1)}) custom-call(bf16[1,4096]{1,0:T(2,128)(2,1)} %q_hbm.1, bf16[1,4096]{1,0:T(2,128)(2,1)} %grad_hbm.1, bf16[1,4096]{1,0:T(2,128)(2,1)} %out_hbm.1, f32[1,32]{1,0:T(1,128)} %lse_hbm.1, bf16[256,128]{1,0:T(8,128)(2,1)} %keys_ref.1, ...), custom_call_target="tpu_custom_call" | custom-call | tf_op jit(solution)/shard_map/attention_backward/pallas_call | solution.py:537
  37.5 0.7 %store_results.1 = (bf16[1,4096]{1,0:T(2,128)(2,1)}, bf16[256,128]{1,0:T(8,128)(2,1)}, bf16[256,128]{1,0:T(8,128)(2,1)}) custom-call(bf16[8,4,128]{2,1,0:T(4,128)(2,1)S(1)} %get-tuple-element.6.dq_ref, bf16[256,128]{1,0:T(8,128)(2,1)S(1)} %get-tuple-element.7.dkeys_ref, bf16[256,128]{1,0:T(8,128)(2,1)S(1)} %get-tuple-element.8.dvalues_ref), custom_call_target="tpu_custom_call" | custom-call | tf_op jit(solution)/shard_map/store_results/pallas_call | solution.py:552

commit v6 on v5

--- a/solution.py
+++ b/solution.py
@@ -392,22 +392,29 @@
         )
 
     for half in (0, 1):
-        axis = 1 - half
         full = jnp.transpose(turned[half][...])
-        dq_full[half][...] = full.reshape(counts[axis], pairs, width)
-        for index in range(counts[axis]):
-            for group in range(groups):
-                first = index * pairs + group * heads
-                dq_away[half][index, group] = full[first : first + heads].astype(jnp.bfloat16)
-        for d in reversed(other_coords(counts[axis])):
-            for group in range(groups):
-                dq_copy(half, around(axis, d), group).start()
+        dq_full[half][...] = full.reshape(counts[1 - half], pairs, width)
+    ready = []
+    for place_of in range(max(counts) - 1):
+        done, ready = ready, []
+        for half in (0, 1):
+            offsets = other_coords(counts[1 - half])[::-1]
+            if place_of < len(offsets):
+                index = around(1 - half, offsets[place_of])
+                rows = dq_full[half][index]
+                for group in range(groups):
+                    dq_away[half][index, group] = rows[group * heads : (group + 1) * heads].astype(jnp.bfloat16)
+                    ready.append(dq_copy(half, index, group))
+        for copy in done:
+            copy.start()
 
     def back_copy(group):
         return remote(
             back.at[group], dq_come[0].at[position[1], mine], send_sem.at[0], back_recv.at[0], (group, place)
         )
 
+    for copy in ready:
+        copy.start()
     own_terms = dq_full[0][position[1]] + dq_full[1][position[0]]
     for group in range(groups):
         back[group] = own_terms[group * heads : (group + 1) * heads].astype(jnp.bfloat16)

time: 38.9 us -> 38.9 us (level)
  no operation moved by 1% of the time
where the time goes in v6:
time: 38.9 us; the launch traced here: 38.2 us
  Pallas kernels  37.6 us (97%)
  between operations  0.64 us (2%)
    pallas_call x1, Pallas kernels, shards(): pl.pallas_call(functools.partial(kernel, (groups, ny, nz, heads, width, h...  36.9 us

profile of v6, /device:TPU:1, one launch (start us, length us, event | category | flops | bytes accessed | tf_op | source)
XLA Modules:
  0.0 38.2 jit_solution(12059773368622740487)
XLA Ops:
  0.6 36.9 %attention_backward.1 = (bf16[8,4,128]{2,1,0:T(4,128)(2,1)S(1)}, bf16[256,128]{1,0:T(8,128)(2,1)S(1)}, bf16[256,128]{1,0:T(8,128)(2,1)S(1)}) custom-call(bf16[1,4096]{1,0:T(2,128)(2,1)} %q_hbm.1, bf16[1,4096]{1,0:T(2,128)(2,1)} %grad_hbm.1, bf16[1,4096]{1,0:T(2,128)(2,1)} %out_hbm.1, f32[1,32]{1,0:T(1,128)} %lse_hbm.1, bf16[256,128]{1,0:T(8,128)(2,1)} %keys_ref.1, ...), custom_call_target="tpu_custom_call" | custom-call | tf_op jit(solution)/shard_map/attention_backward/pallas_call | solution.py:544
  37.5 0.7 %store_results.1 = (bf16[1,4096]{1,0:T(2,128)(2,1)}, bf16[256,128]{1,0:T(8,128)(2,1)}, bf16[256,128]{1,0:T(8,128)(2,1)}) custom-call(bf16[8,4,128]{2,1,0:T(4,128)(2,1)S(1)} %get-tuple-element.6.dq_ref, bf16[256,128]{1,0:T(8,128)(2,1)S(1)} %get-tuple-element.7.dkeys_ref, bf16[256,128]{1,0:T(8,128)(2,1)S(1)} %get-tuple-element.8.dvalues_ref), custom_call_target="tpu_custom_call" | custom-call | tf_op jit(solution)/shard_map/store_results/pallas_call | solution.py:559
